TPU v7x, 32 devices: a whole 2x2x4 slice. The times are simulated.
32 devices in a mesh: blk: 8 (over z, x), grp: 4 (over y, core).
Axes of the slice: x: 2, y: 2, z: 4, core: 2. Of those that a mesh axis runs over, the one named last changes fastest.
Arguments:
- queries: bfloat16 [16384, 512], P(('blk', 'grp')), may hold values from -64 to 64
- keys: bfloat16 [16384, 128], P(('blk', 'grp')), may hold values from -8 to 8
- values: bfloat16 [16384, 128], P(('blk', 'grp')), may hold values from -6 to 6
- selected: int32 [32, 16], replicated, may hold values from 0 to 255, as said below
- key_in: bfloat16 [4096, 256], replicated, may hold values from -0.09375 to 0.09375
- key_out: bfloat16 [256, 128], replicated, may hold values from -0.375 to 0.375
- value_in: bfloat16 [4096, 256], replicated, may hold values from -0.09375 to 0.09375
- value_out: bfloat16 [256, 128], replicated, may hold values from -0.375 to 0.375
- positions: bfloat16 [2, 32, 128], replicated, may hold values from -5 to 5
- gate_weight: bfloat16 [512, 12], replicated, may hold values from -0.25 to 0.25
Outputs:
- attended: bfloat16 [16384, 512], P(('blk', 'grp'))
Inputs may be any that keep to these rules, and one draw needn't show every extreme that they name: `selected`: row d lists 16 different fine blocks. Write r = 32 and b = d // 4. Entry 0 is the first fine block of group d's own tokens. Every listed block j with j // r different from b has j // r < b, and no two listed blocks share a value of j // r other than b. Blocks with j // r == b may lie after group d's tokens.
All inputs are finite; a program needn't handle non-finite values.
Results may differ from a plain program's by a relative error of at most 0.004.
Values may be sent and summed in bfloat16 or wider, within the bound.
A program may use at most 64 MiB of HBM per device.

v0:
```python
import functools
import math

import jax
import jax.numpy as jnp
from jax import lax
from jax.experimental import pallas as pl
from jax.experimental.pallas import tpu as pltpu
from jax.sharding import PartitionSpec as P

HEAD_DIM = 128
HEADS = 4
CMP_BLOCK = 32
SEL_BLOCK = 64
TOPN = 16
WINDOW = 512
ROWS = 128

NEG = -1e30
RATE = HEAD_DIM**-0.5 * math.log2(math.e)
MESH = pl.DeviceIdType.MESH
F32 = jnp.float32
BF16 = jnp.bfloat16


def across(a, b):
    return lax.dot_general(a, b, (((1,), (1,)), ((), ())), preferred_element_type=F32)


def branch(parts, value_parts, floor):
    top = functools.reduce(jnp.maximum, [jnp.max(s, axis=0, keepdims=True) for s in parts])
    total = 0.0
    if floor:
        top = jnp.maximum(top, 0.0)
        total = jnp.exp2(-top * RATE)
    mixed = 0.0
    for s, v in zip(parts, value_parts):
        weights = jnp.exp2((s - top) * RATE)
        total = total + jnp.sum(weights, axis=0, keepdims=True)
        mixed = mixed + jnp.dot(v, weights.astype(BF16), preferred_element_type=F32)
    return mixed, total


def kernel(
    B,
    G,
    sel,
    queries,
    keys,
    values,
    key_in,
    key_out,
    value_in,
    value_out,
    positions,
    gate_weight,
    out,
    w_in,
    w_out,
    shifted,
    sk,
    sv,
    pk,
    pv,
    ik,
    iv,
    stk,
    stv,
    cc,
    cvt,
    wk,
    wvt,
    fk,
    fv,
    fvt,
    ends,
    pool,
    acc,
    gates,
    w_sem,
    a_s,
    a_r,
    m_s,
    m_r,
    p_s,
    p_r,
    b_s,
    b_r,
    c_s,
    c_r,
    f_s,
    f_r,
):
    T = keys.shape[0] * SEL_BLOCK
    N = T // CMP_BLOCK
    Y = G // 2
    per_row = G * T // SEL_BLOCK
    b = lax.axis_index("blk")
    g = lax.axis_index("grp")
    y = g // 2
    core = g % 2
    mate = g + 1 - 2 * core
    position = b * G + g
    first = position * T

    loads = [
        pltpu.make_async_copy(src, dst, w_sem.at[n])
        for n, (src, dst) in enumerate(
            (
                (key_in, w_in.at[0]),
                (value_in, w_in.at[1]),
                (key_out, w_out.at[0]),
                (value_out, w_out.at[1]),
            )
        )
    ]
    for load in loads:
        load.start()

    cc[...] = jnp.zeros_like(cc)
    pk[...] = jnp.zeros_like(pk)
    pv[...] = jnp.zeros_like(pv)

    def remote(src, dst, send, recv, dev):
        return pltpu.make_async_remote_copy(
            src_ref=src,
            dst_ref=dst,
            send_sem=send,
            recv_sem=recv,
            device_id=dev,
            device_id_type=MESH,
        )

    def at(stretch, column):
        return {"blk": stretch, "grp": column}

    last = jnp.logical_and(g == 0, b < B - 1)
    head = jnp.logical_and(g == 0, b > 0)
    barrier = pltpu.get_barrier_semaphore()

    def greet(dev):
        pl.semaphore_signal(barrier, inc=1, device_id=dev, device_id_type=MESH)

    for e in range(1, G):
        greet(at(b, (g + e) % G))
    for d in range(1, B):
        greet(at((b + d) % B, g))

    here = pl.ds(g * (T // SEL_BLOCK), T // SEL_BLOCK)
    sk[here] = keys[...]
    sv[here] = values[...]
    def home(j):
        owner = lax.div(j, per_row)
        return owner, j - owner * per_row

    def same(left, right):
        gap = left - right
        return 1 - jnp.minimum(jnp.maximum(gap, -gap), 1)

    picks = []
    for d in range(1, B):
        line = jnp.minimum(b + d, B - 1) * G + g
        pick = jnp.int32(0)
        for i in range(TOPN):
            owner, rank = home(sel[i, line])
            pick = pick + same(owner, b) * rank
        picks.append(pick)

    gates[...] = jax.nn.sigmoid(
        lax.dot_general(
            gate_weight[...], queries[...], (((1,), (1,)), ((), ())), preferred_element_type=F32
        )
    )

    pl.semaphore_wait(barrier, G - 1 + B - 1)

    own = (keys, values)
    row = (sk, sv)
    prev = (pk, pv)
    staged = (stk, stv)
    inbox = (ik, iv)

    def slot(column):
        return pl.ds(column * (T // SEL_BLOCK), T // SEL_BLOCK)

    def over_y(c, e):
        return remote(
            own[c], row[c].at[slot(g)], a_s.at[c, e], a_r.at[c, e], at(b, ((y + e) % Y) * 2 + core)
        )

    def to_mate(c, e):
        source = ((y - e + Y) % Y) * 2 + core
        src = own[c] if e == 0 else row[c].at[slot(source)]
        return remote(src, row[c].at[slot(source)], m_s.at[c, e], m_r.at[c, e], at(b, mate))

    def to_next(c):
        return remote(
            row[c].at[slot(G - 1)], prev[c], p_s.at[c], p_r.at[c], at((b + 1) % B, 0)
        )

    def block_out(c, d):
        return remote(
            staged[c].at[d - 1], inbox[c].at[b], b_s.at[c, d], b_r.at[c, d], at((b + d) % B, g)
        )

    def coarse_out(d):
        part = cc.at[g, :, pl.ds(pl.multiple_of(b * N, N), N), :]
        return remote(part, part, c_s.at[d], c_r.at[d], at((b + d) % B, g))

    def coarse_over_y(e):
        return remote(
            cc.at[g], cc.at[g], f_s.at[0, e], f_r.at[0, e], at(b, ((y + e) % Y) * 2 + core)
        )

    def coarse_to_mate(e):
        part = cc.at[((y - e + Y) % Y) * 2 + core]
        return remote(part, part, f_s.at[1, e], f_r.at[1, e], at(b, mate))

    for c in range(2):
        for e in range(1, Y):
            over_y(c, e).start()
        to_mate(c, 0).start()

    for c in range(2):
        shift = positions[c].astype(F32)
        shifted[c] = (
            own[c][...].astype(F32).reshape(N, CMP_BLOCK, HEAD_DIM) + shift[None]
        ).reshape(T, HEAD_DIM)
    for load in loads:
        load.wait()
    mine_rows = pl.ds(pl.multiple_of(b * N, N), N)
    for c in range(2):
        flat = jnp.concatenate(
            [shifted[c, pl.ds(t, N, stride=CMP_BLOCK), :].astype(BF16) for t in range(CMP_BLOCK)],
            axis=1,
        )
        hidden = jax.nn.silu(jnp.dot(flat, w_in[c], preferred_element_type=F32)).astype(BF16)
        cc[g, c, mine_rows, :] = jnp.dot(hidden, w_out[c], preferred_element_type=F32).astype(BF16)
    for d in range(1, B):

        @pl.when(b + d < B)
        def _(d=d):
            coarse_out(d).start()

    for e in range(1, Y):
        over_y(0, e).wait_recv()
        to_mate(0, e).start()
    for d in range(1, B):

        @pl.when(b - d >= 0)
        def _(d=d):
            coarse_out(d).wait_recv()

    for e in range(1, Y):
        coarse_over_y(e).start()
    coarse_to_mate(0).start()

    for c in range(2):
        if c == 1:
            for e in range(1, Y):
                over_y(c, e).wait_recv()
                to_mate(c, e).start()
        for e in range(Y):
            to_mate(c, e).wait_recv()
        for d in range(1, B):

            @pl.when(b + d < B)
            def _(c=c, d=d):
                staged[c][d - 1] = row[c][picks[d - 1]]

        for d in range(1, B):

            @pl.when(b + d < B)
            def _(c=c, d=d):
                block_out(c, d).start()

        @pl.when(last)
        def _(c=c):
            to_next(c).start()

    for e in range(1, Y):
        coarse_over_y(e).wait_recv()
        coarse_to_mate(e).start()

    lanes = HEADS * ROWS

    def query_block(start):
        rows = queries[pl.ds(start, ROWS), :]
        return jnp.concatenate(
            [rows[:, h * HEAD_DIM : (h + 1) * HEAD_DIM] for h in range(HEADS)], axis=0
        )

    def gate(n, start):
        return jnp.concatenate(
            [gates[n * HEADS + h : n * HEADS + h + 1, pl.ds(start, ROWS)] for h in range(HEADS)],
            axis=1,
        )

    def iotas(count):
        k = lax.broadcasted_iota(jnp.int32, (count, lanes), 0)
        q = lax.broadcasted_iota(jnp.int32, (count, lanes), 1) % ROWS
        return k, q

    for e in range(Y):
        coarse_to_mate(e).wait_recv()
    for column in range(G):
        cvt[:, pl.ds(column * B * N, B * N)] = cc[column, 1].T

    k, q = iotas(B * N)
    ends[...] = (k // N) * (G * T) + (k % N) * CMP_BLOCK + CMP_BLOCK - 1 - q

    def coarse_step(step, carry):
        start = pl.multiple_of(step * ROWS, ROWS)
        query = query_block(start)
        parts = []
        for column in range(G):
            s = across(cc[column, 0], query)
            parts.append(jnp.where(ends[...] <= first + start - column * T, s, NEG))
        vts = [cvt[:, pl.ds(column * B * N, B * N)] for column in range(G)]
        mixed, total = branch(parts, vts, True)
        acc[step] = mixed * (gate(0, start) / total)
        return carry

    lax.fori_loop(0, T // ROWS, coarse_step, 0, unroll=True)

    @pl.when(head)
    def _():
        for c in range(2):
            to_next(c).wait_recv()

    before = slot(jnp.maximum(g - 1, 0))
    flat = (T, HEAD_DIM)
    wk[pl.ds(0, T), :] = jnp.where(g == 0, pk[...], sk[before]).reshape(flat)
    wk[pl.ds(T, T), :] = keys[...].reshape(flat)
    wvt[:, pl.ds(0, T)] = jnp.where(g == 0, pv[...], sv[before]).reshape(flat).T
    wvt[:, pl.ds(T, T)] = values[...].reshape(flat).T

    def window_step(step, carry):
        start = pl.multiple_of(step * ROWS, ROWS)
        span = pl.ds(pl.multiple_of(start + T - WINDOW, ROWS), ROWS + WINDOW)
        s = across(wk[span, :], query_block(start))
        k, q = iotas(ROWS)
        opening = jnp.where(position == 0, WINDOW - start, 0)
        kk = lax.broadcasted_iota(jnp.int32, (WINDOW - ROWS, lanes), 0) + ROWS
        parts = [
            jnp.where((k > q) & (k >= opening), s[:ROWS], NEG),
            jnp.where(kk >= opening, s[ROWS:WINDOW], NEG),
            jnp.where(k <= q, s[WINDOW:], NEG),
        ]
        vt = wvt[:, span]
        mixed, total = branch(parts, [vt[:, :ROWS], vt[:, ROWS:WINDOW], vt[:, WINDOW:]], False)
        acc[step] = acc[step] + mixed * (gate(2, start) / total)
        return carry

    lax.fori_loop(0, T // ROWS, window_step, 0, unroll=True)

    for c in range(2):
        for d in range(1, B):

            @pl.when(b - d >= 0)
            def _(c=c, d=d):
                block_out(c, d).wait_recv()

    for c in range(2):
        pool[c, :per_row] = row[c][...]
        pool[c, per_row:] = inbox[c][...]
    starts = []
    for i in range(TOPN):
        j = sel[i, position]
        owner, rank = home(j)
        near = same(owner, b)
        entry = near * rank + (1 - near) * (per_row + owner)
        starts.append(j * SEL_BLOCK)
        for c, into in ((0, fk), (1, fv)):
            into[pl.ds(i * SEL_BLOCK, SEL_BLOCK), :] = pool[c, entry]
    fvt[...] = fv[...].T

    def fine_step(step, carry):
        start = pl.multiple_of(step * ROWS, ROWS)
        s = across(fk[...], query_block(start))
        k, q = iotas(SEL_BLOCK)
        ahead = k - q
        parts = [
            jnp.where(
                ahead <= first + start - starts[i], s[i * SEL_BLOCK : (i + 1) * SEL_BLOCK], NEG
            )
            for i in range(TOPN)
        ]
        s = jnp.concatenate(parts, axis=0)
        mixed, total = branch([s], [fvt[...]], False)
        mixed = acc[step] + mixed * (gate(1, start) / total)
        for h in range(HEADS):
            out[pl.ds(start, ROWS), h * HEAD_DIM : (h + 1) * HEAD_DIM] = mixed[
                :, h * ROWS : (h + 1) * ROWS
            ].T.astype(BF16)
        return carry

    lax.fori_loop(0, T // ROWS, fine_step, 0, unroll=True)

    for c in range(2):
        for e in range(1, Y):
            over_y(c, e).wait_send()
        for e in range(Y):
            to_mate(c, e).wait_send()

        @pl.when(last)
        def _(c=c):
            to_next(c).wait_send()

        for d in range(1, B):

            @pl.when(b + d < B)
            def _(c=c, d=d):
                block_out(c, d).wait_send()

    for d in range(1, B):

        @pl.when(b + d < B)
        def _(d=d):
            coarse_out(d).wait_send()

    for e in range(1, Y):
        coarse_over_y(e).wait_send()
    for e in range(Y):
        coarse_to_mate(e).wait_send()


def per_device(
    queries, keys, values, selected, key_in, key_out, value_in, value_out, positions, gate_weight
):
    B = lax.axis_size("blk")
    G = lax.axis_size("grp")
    T = keys.shape[0]
    N = T // CMP_BLOCK
    Y = G // 2
    inner, hidden = key_in.shape
    vmem = pl.BlockSpec(memory_space=pltpu.VMEM)
    smem = pl.BlockSpec(memory_space=pltpu.SMEM)
    hbm = pl.BlockSpec(memory_space=pl.ANY)
    dma = pltpu.SemaphoreType.DMA

    def buf(*shape, dtype=BF16):
        return pltpu.VMEM(shape, dtype)

    return pl.pallas_call(
        functools.partial(kernel, B, G),
        out_shape=jax.ShapeDtypeStruct(queries.shape, BF16),
        in_specs=[smem, vmem, vmem, vmem, hbm, hbm, hbm, hbm, vmem, vmem],
        out_specs=vmem,
        scratch_shapes=[
            buf(2, inner, hidden),
            buf(2, hidden, HEAD_DIM),
            buf(2, T, HEAD_DIM, dtype=F32),
            buf(G * T // SEL_BLOCK, SEL_BLOCK, HEAD_DIM),
            buf(G * T // SEL_BLOCK, SEL_BLOCK, HEAD_DIM),
            buf(T // SEL_BLOCK, SEL_BLOCK, HEAD_DIM),
            buf(T // SEL_BLOCK, SEL_BLOCK, HEAD_DIM),
            buf(B, SEL_BLOCK, HEAD_DIM),
            buf(B, SEL_BLOCK, HEAD_DIM),
            buf(B - 1, SEL_BLOCK, HEAD_DIM),
            buf(B - 1, SEL_BLOCK, HEAD_DIM),
            buf(G, 2, B * N, HEAD_DIM),
            buf(HEAD_DIM, G * B * N),
            buf(2 * T, HEAD_DIM),
            buf(HEAD_DIM, 2 * T),
            buf(TOPN * SEL_BLOCK, HEAD_DIM),
            buf(TOPN * SEL_BLOCK, HEAD_DIM),
            buf(HEAD_DIM, TOPN * SEL_BLOCK),
            buf(B * N, HEADS * ROWS, dtype=jnp.int32),
            buf(2, G * T // SEL_BLOCK + B, SEL_BLOCK, HEAD_DIM),
            buf(T // ROWS, HEAD_DIM, HEADS * ROWS, dtype=F32),
            buf(3 * HEADS, T, dtype=F32),
            dma((4,)),
            dma((2, Y)),
            dma((2, Y)),
            dma((2, Y)),
            dma((2, Y)),
            dma((2,)),
            dma((2,)),
            dma((2, B)),
            dma((2, B)),
            dma((B,)),
            dma((B,)),
            dma((2, Y)),
            dma((2, Y)),
        ],
        compiler_params=pltpu.CompilerParams(
            collective_id=0, has_side_effects=True, vmem_limit_bytes=56 << 20
        ),
    )(
        selected.T,
        queries,
        keys.reshape(T // SEL_BLOCK, SEL_BLOCK, HEAD_DIM),
        values.reshape(T // SEL_BLOCK, SEL_BLOCK, HEAD_DIM),
        key_in,
        key_out,
        value_in,
        value_out,
        positions,
        gate_weight.T,
    )


def solution(mesh):
    rows = P(("blk", "grp"), None)
    return jax.shard_map(
        per_device,
        mesh=mesh,
        in_specs=(rows, rows, rows, P(), P(), P(), P(), P(), P(), P()),
        out_specs=rows,
        check_vma=False,
    )
```

profile of v0, /device:TPU:16, one launch (start us, length us, event | category | flops | bytes accessed | tf_op | source)
XLA Modules:
  0.0 31.3 jit_solution(5658220110780372072)
XLA Ops:
  0.0 29.4 %shard_map.100 = bf16[512,512]{1,0:T(8,128)(2,1)} custom-call(s32[16,32]{1,0:T(8,128)} %bitcast.7, bf16[512,512]{1,0:T(8,128)(2,1)} %queries.1, bf16[8,64,128]{2,1,0:T(8,128)(2,1)} %bitcast.4, bf16[8,64,128]{2,1,0:T(8,128)(2,1)} %bitcast.5, bf16[4096,256]{1,0:T(8,128)(2,1)} %key_in.1, bf16[256,128]{1,0:T(8,128)(2,1)} %key_out.1, bf16[4096,256]{1,0:T(8,128)(2,1)} %value_in.1, ...), custom_call_target="tpu_custom_call" | custom-call | tf_op jit(solution)/shard_map/pallas_call | solution.py:445
  29.4 1.9 %copy.12 = bf16[512,512]{1,0:T(8,128)(2,1)} copy(bf16[512,512]{1,0:T(8,128)(2,1)} %shard_map.100) | data formatting | bytes 1048576
where the time goes:
time: 31.5 us; the launch traced here: 31.3 us
  Pallas kernels  29.4 us (93%)
  local copies, waits for them, and re-layouts  1.87 us (6%)
    pallas_call x1, Pallas kernels, per_device(): pl.pallas_call(functools.partial(kernel, B, G), out_shape=jax.ShapeDtypeS...  29.4 us
    unnamed x1, local copies, waits for them, and re-layouts  1.87 us

commit v1 on v0

v1 whole, which is shorter than its diff:
```python
import functools
import math

import jax
import jax.numpy as jnp
from jax import lax
from jax.experimental import pallas as pl
from jax.experimental.pallas import tpu as pltpu
from jax.sharding import PartitionSpec as P

HEAD_DIM = 128
HEADS = 4
CMP_BLOCK = 32
SEL_BLOCK = 64
TOPN = 16
WINDOW = 512
ROWS = 128
LANES = HEADS * ROWS

FAR = 1e30
RATE = HEAD_DIM**-0.5 * math.log2(math.e)
MESH = pl.DeviceIdType.MESH
F32 = jnp.float32
BF16 = jnp.bfloat16


def across(a, b):
    return lax.dot_general(a, b, (((1,), (1,)), ((), ())), preferred_element_type=F32)


def scores(k, q):
    return across(jnp.concatenate([k, k], axis=1), q)


def rows8(s):
    return s.reshape(s.shape[0] // 8, 8, s.shape[1])


def peak(parts, hides):
    tops = []
    for s, hide in zip(parts, hides):
        top = jnp.max(rows8(s), axis=0)
        tops.append(top if hide is None else top - hide)
    return jnp.max(functools.reduce(jnp.maximum, tops), axis=0, keepdims=True)


def weigh(parts, hides, top):
    packed, sums = [], []
    for s, hide in zip(parts, hides):
        w = jnp.exp2(s - (top if hide is None else top + hide))
        packed.append(w.astype(BF16))
        sums.append(jnp.sum(rows8(w), axis=0))
    total = jnp.sum(functools.reduce(jnp.add, sums), axis=0, keepdims=True)
    return jnp.concatenate(packed, axis=0), total


def times(vt, w):
    return jnp.dot(vt, w, preferred_element_type=F32)


def merge_sort(keys):
    keys = list(keys)
    n = len(keys)
    p = 1
    while p < n:
        k = p
        while k >= 1:
            for j in range(k % p, n - k, 2 * k):
                for i in range(min(k, n - j - k)):
                    if (i + j) // (p * 2) == (i + j + k) // (p * 2):
                        lo, hi = keys[i + j], keys[i + j + k]
                        keys[i + j] = jnp.minimum(lo, hi)
                        keys[i + j + k] = jnp.maximum(lo, hi)
            k //= 2
        p *= 2
    return keys


def kernel(
    B,
    G,
    sel_in,
    queries_in,
    keys_in,
    values_in,
    key_in,
    key_out,
    value_in,
    value_out,
    positions_in,
    gate_weight_in,
    out,
    sel,
    queries,
    positions,
    gate_weight,
    w_in,
    w_out,
    shifted,
    sk,
    sv,
    pk,
    pv,
    ik,
    iv,
    stk,
    stv,
    cc,
    cvt,
    qs,
    wvt,
    pvt,
    fk,
    fvt,
    bias,
    acc,
    part,
    stat,
    gates,
    l_sem,
    w_sem,
    a_s,
    a_r,
    m_s,
    m_r,
    p_s,
    p_r,
    b_s,
    b_r,
    c_s,
    c_r,
    f_s,
    f_r,
    ready,
    ready_head,
):
    T = queries.shape[0]
    N = T // CMP_BLOCK
    Y = G // 2
    STEPS = T // ROWS
    own_blocks = T // SEL_BLOCK
    per_row = G * own_blocks
    near_count = min(max(TOPN - (B - 1), 0), own_blocks)
    b = lax.axis_index("blk")
    g = lax.axis_index("grp")
    y = g // 2
    core = g % 2
    mate = g + 1 - 2 * core
    position = b * G + g
    first = position * T

    row = (sk, sv)
    prev = (pk, pv)
    staged = (stk, stv)
    inbox = (ik, iv)

    def slot(column):
        return pl.ds(column * own_blocks, own_blocks)

    def local(src, dst, sem):
        return pltpu.make_async_copy(src, dst, sem)

    def remote(src, dst, send, recv, dev):
        return pltpu.make_async_remote_copy(
            src_ref=src,
            dst_ref=dst,
            send_sem=send,
            recv_sem=recv,
            device_id=dev,
            device_id_type=MESH,
        )

    def at(stretch, column):
        return {"blk": stretch, "grp": column}

    def when(condition):
        return lambda body: pl.when(condition)(body)

    own_load = [
        local(keys_in, sk.at[slot(g)], l_sem.at[0]),
        local(values_in, sv.at[slot(g)], l_sem.at[1]),
    ]
    q_load = local(queries_in, queries, l_sem.at[2])
    gate_load = local(gate_weight_in, gate_weight, l_sem.at[3])
    shift_load = local(positions_in, positions, l_sem.at[4])
    sel_load = local(sel_in, sel, l_sem.at[5])
    weight_loads = [
        local(src, dst, w_sem.at[n])
        for n, (src, dst) in enumerate(
            (
                (key_in, w_in.at[0]),
                (value_in, w_in.at[1]),
                (key_out, w_out.at[0]),
                (value_out, w_out.at[1]),
            )
        )
    ]
    for load in own_load + [q_load, gate_load, shift_load, sel_load] + weight_loads:
        load.start()

    cc[...] = jnp.zeros_like(cc)
    pk[...] = jnp.zeros_like(pk)
    pv[...] = jnp.zeros_like(pv)

    source = jnp.logical_and(g == 1, b < B - 1)
    head = jnp.logical_and(g == 0, b > 0)
    barrier = pltpu.get_barrier_semaphore()

    def greet(dev):
        pl.semaphore_signal(barrier, inc=1, device_id=dev, device_id_type=MESH)

    for e in range(1, G):
        greet(at(b, (g + e) % G))
    for d in range(1, B):

        @when(b + d < B)
        def _(d=d):
            greet(at(b + d, g))

    @when(source)
    def _():
        greet(at(b + 1, 0))

    pl.semaphore_wait(barrier, G - 1 + b + jnp.where(head, 1, 0))

    def over_y(c, e):
        mine = row[c].at[slot(g)]
        return remote(mine, mine, a_s.at[c, e], a_r.at[c, e], at(b, ((y + e) % Y) * 2 + core))

    def to_mate(c, e):
        piece = row[c].at[slot(((y - e + Y) % Y) * 2 + core)]
        return remote(piece, piece, m_s.at[c, e], m_r.at[c, e], at(b, mate))

    def to_next(c):
        return remote(
            row[c].at[slot(G - 1)], prev[c], p_s.at[c], p_r.at[c], at((b + 1) % B, 0)
        )

    def block_out(c, d):
        return remote(
            staged[c].at[d - 1], inbox[c].at[b], b_s.at[c, d], b_r.at[c, d], at((b + d) % B, g)
        )

    mine_rows = pl.ds(pl.multiple_of(b * N, N), N)

    def coarse_out(d):
        piece = cc.at[g, :, mine_rows, :]
        return remote(piece, piece, c_s.at[d], c_r.at[d], at((b + d) % B, g))

    def coarse_over_y(e):
        return remote(
            cc.at[g], cc.at[g], f_s.at[0, e], f_r.at[0, e], at(b, ((y + e) % Y) * 2 + core)
        )

    def coarse_to_mate(e):
        piece = cc.at[((y - e + Y) % Y) * 2 + core]
        return remote(piece, piece, f_s.at[1, e], f_r.at[1, e], at(b, mate))

    for c in range(2):
        own_load[c].wait()
        for e in range(1, Y):
            over_y(c, e).start()
        to_mate(c, 0).start()

    for d in range(1, B):

        @when(b - d >= 0)
        def _(d=d):
            pl.semaphore_signal(ready.at[d], inc=1, device_id=at(b - d, g), device_id_type=MESH)

    @when(head)
    def _():
        pl.semaphore_signal(ready_head, inc=1, device_id=at(b - 1, 1), device_id_type=MESH)

    q_load.wait()
    for step in range(STEPS):
        for h in range(HEADS):
            piece = queries[step * ROWS : (step + 1) * ROWS, h * HEAD_DIM : (h + 1) * HEAD_DIM]
            piece = piece.astype(F32) * RATE
            high = piece.astype(BF16)
            qs[step, h * ROWS : (h + 1) * ROWS, :HEAD_DIM] = high
            qs[step, h * ROWS : (h + 1) * ROWS, HEAD_DIM:] = (piece - high.astype(F32)).astype(BF16)
    gate_load.wait()
    gates[...] = jax.nn.sigmoid(across(gate_weight[...], queries[...]))

    shift_load.wait()
    flat = (T, HEAD_DIM)
    for c in range(2):
        shift = positions[c].astype(F32)
        tokens = row[c][slot(g)].reshape(flat).astype(F32).reshape(N, CMP_BLOCK, HEAD_DIM)
        shifted[c] = (tokens + shift[None]).reshape(flat)
    wvt[...] = sv[slot(g)].reshape(flat).T
    for load in weight_loads:
        load.wait()
    for c in range(2):
        wide = jnp.concatenate(
            [shifted[c, pl.ds(t, N, stride=CMP_BLOCK), :].astype(BF16) for t in range(CMP_BLOCK)],
            axis=1,
        )
        hidden = jax.nn.silu(jnp.dot(wide, w_in[c], preferred_element_type=F32)).astype(BF16)
        cc[g, c, mine_rows, :] = jnp.dot(hidden, w_out[c], preferred_element_type=F32).astype(BF16)

    sel_load.wait()

    def owner_of(j):
        return lax.div(j, per_row)

    def same(left, right):
        gap = left - right
        return 1 - jnp.minimum(jnp.maximum(gap, -gap), 1)

    picks = []
    for d in range(1, B):
        line = jnp.minimum(b + d, B - 1) * G + g
        pick = jnp.int32(0)
        for i in range(TOPN):
            j = sel[i, line]
            pick = pick + same(owner_of(j), b) * (j - b * per_row)
        picks.append(pick)

    order = []
    for i in range(TOPN):
        j = sel[i, position]
        rel = j - b * per_row - g * own_blocks
        wrapped = jnp.where(rel < 0, rel + per_row, rel)
        order.append(jnp.where(j >= b * per_row, wrapped, j + per_row))
    order = merge_sort(order)

    def entry(i):
        code = order[i]
        near = code < per_row
        turned = code + g * own_blocks
        rank = jnp.where(turned >= per_row, turned - per_row, turned)
        rank = jnp.where(near, rank, 0)
        start = jnp.where(near, (b * per_row + rank) * SEL_BLOCK, 0)
        owner = jnp.where(near, 0, owner_of(code - per_row))
        return near, rank, owner, start

    def iotas(count):
        k = lax.broadcasted_iota(jnp.int32, (count, LANES), 0)
        q = lax.broadcasted_iota(jnp.int32, (count, LANES), 1) % ROWS
        return k, q

    def gate(n, step):
        cols = pl.ds(step * ROWS, ROWS)
        return jnp.concatenate(
            [gates[n * HEADS + h : n * HEADS + h + 1, cols] for h in range(HEADS)], axis=1
        )

    def keep(which, step, mixed, top, total):
        part[which, step] = mixed
        stat[which, step, 0:1] = top
        stat[which, step, 1:2] = total

    def join(which, step, mixed, top, total, best):
        old = jnp.exp2(stat[which, step, 0:1] - best)
        return part[which, step] * old + mixed, stat[which, step, 1:2] * old + total

    kd, qd = iotas(ROWS)
    own_keys = sk[slot(g)].reshape(flat)
    for step in range(STEPS):
        count = (step + 1) * ROWS
        s = scores(own_keys[:count], qs[step])
        parts = [jnp.where(kd <= qd, s[count - ROWS :], -FAR)]
        if step > 0:
            parts = [s[: count - ROWS]] + parts
        hides = [None] * len(parts)
        top = peak(parts, hides)
        w, total = weigh(parts, hides, top)
        keep(0, step, times(wvt[:, :count], w), top, total)

    for d in range(B - 1, 0, -1):

        @when(b + d < B)
        def _(d=d):
            pl.semaphore_wait(ready.at[d], 1)
            coarse_out(d).start()

    @when(source)
    def _():
        pl.semaphore_wait(ready_head, 1)

    def relay(c):
        for e in range(1, Y):
            over_y(c, e).wait_recv()
            to_mate(c, e).start()

        @when(source)
        def _():
            to_next(c).start()

    def spread(c):
        for e in range(Y):
            to_mate(c, e).wait_recv()
        for d in range(B - 1, 0, -1):

            @when(b + d < B)
            def _(d=d):
                staged[c][d - 1] = row[c][picks[d - 1]]

        for d in range(B - 1, 0, -1):

            @when(b + d < B)
            def _(d=d):
                block_out(c, d).start()

    relay(0)

    for d in range(1, B):

        @when(b - d >= 0)
        def _(d=d):
            coarse_out(d).wait_recv()

    for e in range(1, Y):
        coarse_over_y(e).start()
    coarse_to_mate(0).start()

    spread(0)

    entries = [entry(i) for i in range(TOPN)]
    for i in range(near_count):
        fk[pl.ds(i * SEL_BLOCK, SEL_BLOCK), :] = sk[entries[i][1]]

    for e in range(1, Y):
        coarse_over_y(e).wait_recv()
        coarse_to_mate(e).start()

    relay(1)

    for e in range(Y):
        coarse_to_mate(e).wait_recv()

    for column in range(G):
        cvt[:, pl.ds(column * B * N, B * N)] = cc[column, 1].T
    cvt[:, pl.ds(G * B * N, ROWS)] = jnp.concatenate(
        [cc[g, 1, mine_rows, :], jnp.zeros((ROWS - N, HEAD_DIM), BF16)], axis=0
    ).T
    k = lax.broadcasted_iota(jnp.int32, (B * N, ROWS), 0)
    for column in range(G):
        seen = (k // N) * G + column < position
        bias[pl.ds(column * B * N, B * N), :] = jnp.where(seen, 0.0, -FAR)
    kc, qc = iotas(N)
    ends = kc * CMP_BLOCK + (CMP_BLOCK - 1) - qc

    def coarse_step(step, carry):
        parts = []
        for column in range(G):
            s = scores(cc[column, 0], qs[step])
            off = bias[pl.ds(column * B * N, B * N), :]
            parts.append(s + jnp.concatenate([off] * HEADS, axis=1))
        s = scores(cc[g, 0, mine_rows, :], qs[step])
        parts.append(jnp.where(ends <= step * ROWS, s, -FAR))
        hides = [None] * len(parts)
        top = jnp.maximum(peak(parts, hides), 0.0)
        w, total = weigh(parts, hides, top)
        w = jnp.concatenate([w, jnp.zeros((ROWS - N, LANES), BF16)], axis=0)
        total = total + jnp.exp2(-top)
        acc[step] = times(cvt[...], w) * (gate(0, step) / total)
        return carry

    half = STEPS // 2
    lax.fori_loop(0, half, coarse_step, 0, unroll=True)
    spread(1)
    lax.fori_loop(half, STEPS, coarse_step, 0, unroll=True)

    ks, qf = iotas(SEL_BLOCK)
    ahead = ks - qf

    def fine_parts(step, low, high):
        s = scores(fk[pl.ds(low * SEL_BLOCK, (high - low) * SEL_BLOCK), :], qs[step])
        parts, hides = [], []
        for i in range(low, high):
            piece = s[(i - low) * SEL_BLOCK : (i - low + 1) * SEL_BLOCK]
            start = entries[i][3]
            if i < own_blocks:
                parts.append(jnp.where(ahead <= first + step * ROWS - start, piece, -FAR))
                hides.append(None)
            else:
                parts.append(piece)
                hides.append(jnp.where(start <= first, 0.0, FAR).astype(F32))
        return parts, hides

    if near_count > 0:
        for i in range(near_count):
            fvt[:, pl.ds(i * SEL_BLOCK, SEL_BLOCK)] = sv[entries[i][1]].T

        def near_step(step, carry):
            parts, hides = fine_parts(step, 0, near_count)
            top = peak(parts, hides)
            w, total = weigh(parts, hides, top)
            keep(1, step, times(fvt[:, : near_count * SEL_BLOCK], w), top, total)
            return carry

        lax.fori_loop(0, STEPS, near_step, 0, unroll=True)

    @when(head)
    def _():
        for c in range(2):
            to_next(c).wait_recv()

    before = slot(jnp.maximum(g - 1, 0))
    prev_keys = jnp.where(g == 0, pk[...], sk[before]).reshape(flat)
    pvt[...] = jnp.where(g == 0, pv[...], sv[before]).reshape(flat).T
    opening = jnp.where(position == 0, FAR, 0.0).astype(F32)
    for step in range(STEPS):
        low = step * ROWS
        s = scores(prev_keys[low:], qs[step])
        parts = [jnp.where(kd > qd, s[:ROWS], -FAR)]
        if step < STEPS - 1:
            parts.append(s[ROWS:])
        hides = [opening] * len(parts)
        top = jnp.maximum(peak(parts, hides), stat[0, step, 0:1])
        w, total = weigh(parts, hides, top)
        mixed, total = join(0, step, times(pvt[:, low:], w), top, total, top)
        acc[step] = acc[step] + mixed * (gate(2, step) / total)

    for c in range(2):
        for d in range(1, B):

            @when(b - d >= 0)
            def _(c=c, d=d):
                block_out(c, d).wait_recv()

    for i in range(near_count, TOPN):
        near, rank, owner, _ = entries[i]
        fk[pl.ds(i * SEL_BLOCK, SEL_BLOCK), :] = jnp.where(near, sk[rank], ik[owner])
        fvt[:, pl.ds(i * SEL_BLOCK, SEL_BLOCK)] = jnp.where(near, sv[rank], iv[owner]).T

    def far_step(step, carry):
        parts, hides = fine_parts(step, near_count, TOPN)
        top = peak(parts, hides)
        if near_count > 0:
            top = jnp.maximum(top, stat[1, step, 0:1])
        w, total = weigh(parts, hides, top)
        mixed = times(fvt[:, near_count * SEL_BLOCK :], w)
        if near_count > 0:
            mixed, total = join(1, step, mixed, top, total, top)
        mixed = acc[step] + mixed * (gate(1, step) / total)
        for h in range(HEADS):
            out[pl.ds(step * ROWS, ROWS), h * HEAD_DIM : (h + 1) * HEAD_DIM] = mixed[
                :, h * ROWS : (h + 1) * ROWS
            ].T.astype(BF16)
        return carry

    lax.fori_loop(0, STEPS, far_step, 0, unroll=True)

    for c in range(2):
        for e in range(1, Y):
            over_y(c, e).wait_send()
        for e in range(Y):
            to_mate(c, e).wait_send()

        @when(source)
        def _(c=c):
            to_next(c).wait_send()

        for d in range(1, B):

            @when(b + d < B)
            def _(c=c, d=d):
                block_out(c, d).wait_send()

    for d in range(1, B):

        @when(b + d < B)
        def _(d=d):
            coarse_out(d).wait_send()

    for e in range(1, Y):
        coarse_over_y(e).wait_send()
    for e in range(Y):
        coarse_to_mate(e).wait_send()


def per_device(
    queries, keys, values, selected, key_in, key_out, value_in, value_out, positions, gate_weight
):
    B = lax.axis_size("blk")
    G = lax.axis_size("grp")
    T = keys.shape[0]
    N = T // CMP_BLOCK
    Y = G // 2
    STEPS = T // ROWS
    own_blocks = T // SEL_BLOCK
    inner, hidden = key_in.shape
    anywhere = pl.BlockSpec(memory_space=pl.ANY)
    dma = pltpu.SemaphoreType.DMA
    regular = pltpu.SemaphoreType.REGULAR

    def buf(*shape, dtype=BF16):
        return pltpu.VMEM(shape, dtype)

    def blocks(count):
        return buf(count, SEL_BLOCK, HEAD_DIM)

    return pl.pallas_call(
        functools.partial(kernel, B, G),
        out_shape=pltpu.VMEM(queries.shape, BF16),
        in_specs=[anywhere] * 10,
        out_specs=pl.BlockSpec(memory_space=pltpu.VMEM),
        scratch_shapes=[
            pltpu.SMEM((TOPN, B * G), jnp.int32),
            buf(*queries.shape),
            buf(*positions.shape),
            buf(gate_weight.shape[1], gate_weight.shape[0]),
            buf(2, inner, hidden),
            buf(2, hidden, HEAD_DIM),
            buf(2, T, HEAD_DIM, dtype=F32),
            blocks(G * own_blocks),
            blocks(G * own_blocks),
            blocks(own_blocks),
            blocks(own_blocks),
            blocks(B),
            blocks(B),
            blocks(B - 1),
            blocks(B - 1),
            buf(G, 2, B * N, HEAD_DIM),
            buf(HEAD_DIM, G * B * N + ROWS),
            buf(STEPS, LANES, 2 * HEAD_DIM),
            buf(HEAD_DIM, T),
            buf(HEAD_DIM, T),
            buf(TOPN * SEL_BLOCK, HEAD_DIM),
            buf(HEAD_DIM, TOPN * SEL_BLOCK),
            buf(G * B * N, ROWS, dtype=F32),
            buf(STEPS, HEAD_DIM, LANES, dtype=F32),
            buf(2, STEPS, HEAD_DIM, LANES, dtype=F32),
            buf(2, STEPS, 8, LANES, dtype=F32),
            buf(3 * HEADS, T, dtype=F32),
            dma((6,)),
            dma((4,)),
            dma((2, Y)),
            dma((2, Y)),
            dma((2, Y)),
            dma((2, Y)),
            dma((2,)),
            dma((2,)),
            dma((2, B)),
            dma((2, B)),
            dma((B,)),
            dma((B,)),
            dma((2, Y)),
            dma((2, Y)),
            regular((B,)),
            regular,
        ],
        compiler_params=pltpu.CompilerParams(
            collective_id=0, has_side_effects=True, vmem_limit_bytes=56 << 20
        ),
    )(
        selected.T,
        queries,
        keys.reshape(T // SEL_BLOCK, SEL_BLOCK, HEAD_DIM),
        values.reshape(T // SEL_BLOCK, SEL_BLOCK, HEAD_DIM),
        key_in,
        key_out,
        value_in,
        value_out,
        positions,
        gate_weight.T,
    )


def solution(mesh):
    rows = P(("blk", "grp"), None)
    return jax.shard_map(
        per_device,
        mesh=mesh,
        in_specs=(rows, rows, rows, P(), P(), P(), P(), P(), P(), P()),
        out_specs=rows,
        check_vma=False,
    )
```

time: 31.5 us -> 25.8 us (0.82)
  the two profiles are of different devices: /device:TPU:16 before, /device:TPU:17 now
where the time goes in v1:
time: 25.8 us; the launch traced here: 25.7 us
  Pallas kernels  24.9 us (97%)
  local copies, waits for them, and re-layouts  0.8 us (3%)
    pallas_call x1, Pallas kernels, per_device(): pl.pallas_call(functools.partial(kernel, B, G), out_shape=pltpu.VMEM(quer...  24.9 us
    unnamed x1, local copies, waits for them, and re-layouts  0.8 us

profile of v1, /device:TPU:17, one launch (start us, length us, event | category | flops | bytes accessed | tf_op | source)
XLA Modules:
  0.0 25.7 jit_solution(7782572719452015888)
XLA Ops:
  0.0 24.9 %shard_map.100 = bf16[512,512]{1,0:T(8,128)(2,1)S(1)} custom-call(s32[16,32]{1,0:T(8,128)} %bitcast.7, bf16[512,512]{1,0:T(8,128)(2,1)} %queries_in.1, bf16[8,64,128]{2,1,0:T(8,128)(2,1)} %bitcast.4, bf16[8,64,128]{2,1,0:T(8,128)(2,1)} %bitcast.5, bf16[4096,256]{1,0:T(8,128)(2,1)} %key_in.1, bf16[256,128]{1,0:T(8,128)(2,1)} %key_out.1, ...), custom_call_target="tpu_custom_call" | custom-call | tf_op jit(solution)/shard_map/pallas_call | solution.py:597
  24.9 0.8 %copy.12 = bf16[512,512]{1,0:T(8,128)(2,1)} copy(bf16[512,512]{1,0:T(8,128)(2,1)S(1)} %shard_map.100) | data formatting | bytes 1048576

commit v2 on v1

--- a/solution.py
+++ b/solution.py
@@ -29,7 +29,7 @@
 
 
 def scores(k, q):
-    return across(jnp.concatenate([k, k], axis=1), q)
+    return jnp.dot(jnp.concatenate([k, k], axis=1), q, preferred_element_type=F32)
 
 
 def rows8(s):
@@ -56,6 +56,14 @@
 
 def times(vt, w):
     return jnp.dot(vt, w, preferred_element_type=F32)
+
+
+def pipeline(fronts, backs):
+    held = fronts[0]()
+    for n, back in enumerate(backs):
+        following = fronts[n + 1]() if n + 1 < len(fronts) else None
+        back(*held)
+        held = following
 
 
 def merge_sort(keys):
@@ -113,6 +121,7 @@
     fk,
     fvt,
     bias,
+    wnear,
     acc,
     part,
     stat,
@@ -132,7 +141,6 @@
     f_s,
     f_r,
     ready,
-    ready_head,
 ):
     T = queries.shape[0]
     N = T // CMP_BLOCK
@@ -203,7 +211,6 @@
     pv[...] = jnp.zeros_like(pv)
 
     source = jnp.logical_and(g == 1, b < B - 1)
-    head = jnp.logical_and(g == 0, b > 0)
     barrier = pltpu.get_barrier_semaphore()
 
     def greet(dev):
@@ -217,23 +224,27 @@
         def _(d=d):
             greet(at(b + d, g))
 
-    @when(source)
-    def _():
-        greet(at(b + 1, 0))
-
-    pl.semaphore_wait(barrier, G - 1 + b + jnp.where(head, 1, 0))
-
-    def over_y(c, e):
-        mine = row[c].at[slot(g)]
-        return remote(mine, mine, a_s.at[c, e], a_r.at[c, e], at(b, ((y + e) % Y) * 2 + core))
-
-    def to_mate(c, e):
-        piece = row[c].at[slot(((y - e + Y) % Y) * 2 + core)]
-        return remote(piece, piece, m_s.at[c, e], m_r.at[c, e], at(b, mate))
-
-    def to_next(c):
+    pl.semaphore_wait(barrier, G - 1 + b)
+
+    def piece_of(column, h):
+        return pl.ds(column * own_blocks + h * (own_blocks // 2), own_blocks // 2)
+
+    def over_y(c, e, h):
+        piece = row[c].at[piece_of(g, h)]
+        dev = at(b, ((y + e) % Y) * 2 + core)
+        return remote(piece, piece, a_s.at[c, e, h], a_r.at[c, e, h], dev)
+
+    def to_mate(c, e, h):
+        piece = row[c].at[piece_of(((y - e + Y) % Y) * 2 + core, h)]
+        return remote(piece, piece, m_s.at[c, e, h], m_r.at[c, e, h], at(b, mate))
+
+    def to_next(c, h):
         return remote(
-            row[c].at[slot(G - 1)], prev[c], p_s.at[c], p_r.at[c], at((b + 1) % B, 0)
+            row[c].at[piece_of(G - 1, h)],
+            prev[c].at[piece_of(0, h)],
+            p_s.at[c, h],
+            p_r.at[c, h],
+            at((b + 1) % B, 0),
         )
 
     def block_out(c, d):
@@ -241,47 +252,48 @@
             staged[c].at[d - 1], inbox[c].at[b], b_s.at[c, d], b_r.at[c, d], at((b + d) % B, g)
         )
 
-    mine_rows = pl.ds(pl.multiple_of(b * N, N), N)
+    mine_rows = pl.ds(pl.multiple_of((g * B + b) * N, N), N)
+
+    def column_rows(column):
+        return pl.ds(pl.multiple_of(column * B * N, N), B * N)
 
     def coarse_out(d):
-        piece = cc.at[g, :, mine_rows, :]
+        piece = cc.at[:, mine_rows, :]
         return remote(piece, piece, c_s.at[d], c_r.at[d], at((b + d) % B, g))
 
     def coarse_over_y(e):
-        return remote(
-            cc.at[g], cc.at[g], f_s.at[0, e], f_r.at[0, e], at(b, ((y + e) % Y) * 2 + core)
-        )
+        piece = cc.at[:, column_rows(g), :]
+        dev = at(b, ((y + e) % Y) * 2 + core)
+        return remote(piece, piece, f_s.at[0, e], f_r.at[0, e], dev)
 
     def coarse_to_mate(e):
-        piece = cc.at[((y - e + Y) % Y) * 2 + core]
+        piece = cc.at[:, column_rows(((y - e + Y) % Y) * 2 + core), :]
         return remote(piece, piece, f_s.at[1, e], f_r.at[1, e], at(b, mate))
 
-    for c in range(2):
-        own_load[c].wait()
+    halves = range(2)
+    own_load[0].wait()
+    for h in halves:
         for e in range(1, Y):
-            over_y(c, e).start()
-        to_mate(c, 0).start()
+            over_y(0, e, h).start()
+        to_mate(0, 0, h).start()
+    own_load[1].wait()
+    for h in halves:
+        to_mate(1, 0, h).start()
 
     for d in range(1, B):
 
         @when(b - d >= 0)
         def _(d=d):
             pl.semaphore_signal(ready.at[d], inc=1, device_id=at(b - d, g), device_id_type=MESH)
-
-    @when(head)
-    def _():
-        pl.semaphore_signal(ready_head, inc=1, device_id=at(b - 1, 1), device_id_type=MESH)
 
     q_load.wait()
     for step in range(STEPS):
         for h in range(HEADS):
             piece = queries[step * ROWS : (step + 1) * ROWS, h * HEAD_DIM : (h + 1) * HEAD_DIM]
-            piece = piece.astype(F32) * RATE
+            piece = piece.T.astype(F32) * RATE
             high = piece.astype(BF16)
-            qs[step, h * ROWS : (h + 1) * ROWS, :HEAD_DIM] = high
-            qs[step, h * ROWS : (h + 1) * ROWS, HEAD_DIM:] = (piece - high.astype(F32)).astype(BF16)
-    gate_load.wait()
-    gates[...] = jax.nn.sigmoid(across(gate_weight[...], queries[...]))
+            qs[step, :HEAD_DIM, h * ROWS : (h + 1) * ROWS] = high
+            qs[step, HEAD_DIM:, h * ROWS : (h + 1) * ROWS] = (piece - high.astype(F32)).astype(BF16)
 
     shift_load.wait()
     flat = (T, HEAD_DIM)
@@ -298,8 +310,80 @@
             axis=1,
         )
         hidden = jax.nn.silu(jnp.dot(wide, w_in[c], preferred_element_type=F32)).astype(BF16)
-        cc[g, c, mine_rows, :] = jnp.dot(hidden, w_out[c], preferred_element_type=F32).astype(BF16)
-
+        mine = jnp.dot(hidden, w_out[c], preferred_element_type=F32).astype(BF16)
+        cc[c, mine_rows, :] = mine
+        cc[c, G * B * N : G * B * N + N, :] = mine
+    for h in halves:
+        for e in range(1, Y):
+            over_y(1, e, h).start()
+
+    def coarse_on(low, high):
+        for d in range(low, high):
+
+            @when(b + d < B)
+            def _(d=d):
+                pl.semaphore_wait(ready.at[d], 1)
+                coarse_out(d).start()
+
+    coarse_on(1, B // 2)
+
+    def iotas(count):
+        k = lax.broadcasted_iota(jnp.int32, (count, LANES), 0)
+        q = lax.broadcasted_iota(jnp.int32, (count, LANES), 1) % ROWS
+        return k, q
+
+    def gate(n, step):
+        cols = pl.ds(step * ROWS, ROWS)
+        return jnp.concatenate(
+            [gates[n * HEADS + h : n * HEADS + h + 1, cols] for h in range(HEADS)], axis=1
+        )
+
+    def keep(which, step, mixed, top, total):
+        part[which, step] = mixed
+        stat[which, step, 0:1] = top
+        stat[which, step, 1:2] = total
+
+    def join(which, step, mixed, total, best):
+        old = jnp.exp2(stat[which, step, 0:1] - best)
+        return part[which, step] * old + mixed, stat[which, step, 1:2] * old + total
+
+    kd, qd = iotas(ROWS)
+    own_keys = sk[slot(g)].reshape(flat)
+
+    def own_front(step):
+        count = (step + 1) * ROWS
+        s = scores(own_keys[:count], qs[step])
+        parts = [jnp.where(kd <= qd, s[count - ROWS :], -FAR)]
+        if step > 0:
+            parts = [s[: count - ROWS]] + parts
+        hides = [None] * len(parts)
+        return parts, hides, peak(parts, hides)
+
+    def own_back(step, parts, hides, top):
+        w, total = weigh(parts, hides, top)
+        keep(0, step, times(wvt[:, : (step + 1) * ROWS], w), top, total)
+
+    def spans(front, back):
+        return (
+            [functools.partial(front, step) for step in range(STEPS)],
+            [functools.partial(back, step) for step in range(STEPS)],
+        )
+
+    pipeline(*spans(own_front, own_back))
+    coarse_on(B // 2, B)
+
+    def relay(c, h):
+        for e in range(1, Y):
+            over_y(c, e, h).wait_recv()
+            to_mate(c, e, h).start()
+
+        @when(source)
+        def _():
+            to_next(c, h).start()
+
+    relay(0, 0)
+    gate_load.wait()
+    gates[...] = jax.nn.sigmoid(across(gate_weight[...], queries[...]))
     sel_load.wait()
 
     def owner_of(j):
@@ -336,62 +420,10 @@
         owner = jnp.where(near, 0, owner_of(code - per_row))
         return near, rank, owner, start
 
-    def iotas(count):
-        k = lax.broadcasted_iota(jnp.int32, (count, LANES), 0)
-        q = lax.broadcasted_iota(jnp.int32, (count, LANES), 1) % ROWS
-        return k, q
-
-    def gate(n, step):
-        cols = pl.ds(step * ROWS, ROWS)
-        return jnp.concatenate(
-            [gates[n * HEADS + h : n * HEADS + h + 1, cols] for h in range(HEADS)], axis=1
-        )
-
-    def keep(which, step, mixed, top, total):
-        part[which, step] = mixed
-        stat[which, step, 0:1] = top
-        stat[which, step, 1:2] = total
-
-    def join(which, step, mixed, top, total, best):
-        old = jnp.exp2(stat[which, step, 0:1] - best)
-        return part[which, step] * old + mixed, stat[which, step, 1:2] * old + total
-
-    kd, qd = iotas(ROWS)
-    own_keys = sk[slot(g)].reshape(flat)
-    for step in range(STEPS):
-        count = (step + 1) * ROWS
-        s = scores(own_keys[:count], qs[step])
-        parts = [jnp.where(kd <= qd, s[count - ROWS :], -FAR)]
-        if step > 0:
-            parts = [s[: count - ROWS]] + parts
-        hides = [None] * len(parts)
-        top = peak(parts, hides)
-        w, total = weigh(parts, hides, top)
-        keep(0, step, times(wvt[:, :count], w), top, total)
-
-    for d in range(B - 1, 0, -1):
-
-        @when(b + d < B)
-        def _(d=d):
-            pl.semaphore_wait(ready.at[d], 1)
-            coarse_out(d).start()
-
-    @when(source)
-    def _():
-        pl.semaphore_wait(ready_head, 1)
-
-    def relay(c):
-        for e in range(1, Y):
-            over_y(c, e).wait_recv()
-            to_mate(c, e).start()
-
-        @when(source)
-        def _():
-            to_next(c).start()
-
     def spread(c):
         for e in range(Y):
-            to_mate(c, e).wait_recv()
+            for h in halves:
+                to_mate(c, e, h).wait_recv()
         for d in range(B - 1, 0, -1):
 
             @when(b + d < B)
@@ -404,7 +436,7 @@
             def _(d=d):
                 block_out(c, d).start()
 
-    relay(0)
+    relay(0, 1)
 
     for d in range(1, B):
 
@@ -421,48 +453,6 @@
     entries = [entry(i) for i in range(TOPN)]
     for i in range(near_count):
         fk[pl.ds(i * SEL_BLOCK, SEL_BLOCK), :] = sk[entries[i][1]]
-
-    for e in range(1, Y):
-        coarse_over_y(e).wait_recv()
-        coarse_to_mate(e).start()
-
-    relay(1)
-
-    for e in range(Y):
-        coarse_to_mate(e).wait_recv()
-
-    for column in range(G):
-        cvt[:, pl.ds(column * B * N, B * N)] = cc[column, 1].T
-    cvt[:, pl.ds(G * B * N, ROWS)] = jnp.concatenate(
-        [cc[g, 1, mine_rows, :], jnp.zeros((ROWS - N, HEAD_DIM), BF16)], axis=0
-    ).T
-    k = lax.broadcasted_iota(jnp.int32, (B * N, ROWS), 0)
-    for column in range(G):
-        seen = (k // N) * G + column < position
-        bias[pl.ds(column * B * N, B * N), :] = jnp.where(seen, 0.0, -FAR)
-    kc, qc = iotas(N)
-    ends = kc * CMP_BLOCK + (CMP_BLOCK - 1) - qc
-
-    def coarse_step(step, carry):
-        parts = []
-        for column in range(G):
-            s = scores(cc[column, 0], qs[step])
-            off = bias[pl.ds(column * B * N, B * N), :]
-            parts.append(s + jnp.concatenate([off] * HEADS, axis=1))
-        s = scores(cc[g, 0, mine_rows, :], qs[step])
-        parts.append(jnp.where(ends <= step * ROWS, s, -FAR))
-        hides = [None] * len(parts)
-        top = jnp.maximum(peak(parts, hides), 0.0)
-        w, total = weigh(parts, hides, top)
-        w = jnp.concatenate([w, jnp.zeros((ROWS - N, LANES), BF16)], axis=0)
-        total = total + jnp.exp2(-top)
-        acc[step] = times(cvt[...], w) * (gate(0, step) / total)
-        return carry
-
-    half = STEPS // 2
-    lax.fori_loop(0, half, coarse_step, 0, unroll=True)
-    spread(1)
-    lax.fori_loop(half, STEPS, coarse_step, 0, unroll=True)
 
     ks, qf = iotas(SEL_BLOCK)
     ahead = ks - qf
@@ -481,39 +471,98 @@
                 hides.append(jnp.where(start <= first, 0.0, FAR).astype(F32))
         return parts, hides
 
+    def near_front(step):
+        parts, hides = fine_parts(step, 0, near_count)
+        return parts, hides, peak(parts, hides)
+
+    def near_back(step, parts, hides, top):
+        w, total = weigh(parts, hides, top)
+        wnear[step] = w
+        stat[1, step, 0:1] = top
+        stat[1, step, 1:2] = total
+
+    half = STEPS // 2
+    if near_count > 0:
+        near_fronts, near_backs = spans(near_front, near_back)
+        pipeline(near_fronts[:half], near_backs[:half])
+    relay(1, 0)
+    if near_count > 0:
+        pipeline(near_fronts[half:], near_backs[half:])
+    relay(1, 1)
+    spread(1)
+
     if near_count > 0:
         for i in range(near_count):
             fvt[:, pl.ds(i * SEL_BLOCK, SEL_BLOCK)] = sv[entries[i][1]].T
-
-        def near_step(step, carry):
-            parts, hides = fine_parts(step, 0, near_count)
-            top = peak(parts, hides)
+        for step in range(STEPS):
+            part[1, step] = times(fvt[:, : near_count * SEL_BLOCK], wnear[step])
+
+    for e in range(1, Y):
+        coarse_over_y(e).wait_recv()
+        coarse_to_mate(e).start()
+
+    def prev_phase(prev_keys, opening):
+        def prev_front(step):
+            s = scores(prev_keys[step * ROWS :], qs[step])
+            parts = [jnp.where(kd > qd, s[:ROWS], -FAR)]
+            if step < STEPS - 1:
+                parts.append(s[ROWS:])
+            hides = [opening] * len(parts)
+            return parts, hides, jnp.maximum(peak(parts, hides), stat[0, step, 0:1])
+
+        def prev_back(step, parts, hides, top):
             w, total = weigh(parts, hides, top)
-            keep(1, step, times(fvt[:, : near_count * SEL_BLOCK], w), top, total)
-            return carry
-
-        lax.fori_loop(0, STEPS, near_step, 0, unroll=True)
-
-    @when(head)
+            mixed = times(pvt[:, step * ROWS :], w)
+            mixed, total = join(0, step, mixed, total, top)
+            part[0, step] = mixed * (gate(2, step) / total)
+
+        pipeline(*spans(prev_front, prev_back))
+
+    @when(g > 0)
     def _():
-        for c in range(2):
-            to_next(c).wait_recv()
-
-    before = slot(jnp.maximum(g - 1, 0))
-    prev_keys = jnp.where(g == 0, pk[...], sk[before]).reshape(flat)
-    pvt[...] = jnp.where(g == 0, pv[...], sv[before]).reshape(flat).T
-    opening = jnp.where(position == 0, FAR, 0.0).astype(F32)
-    for step in range(STEPS):
-        low = step * ROWS
-        s = scores(prev_keys[low:], qs[step])
-        parts = [jnp.where(kd > qd, s[:ROWS], -FAR)]
-        if step < STEPS - 1:
-            parts.append(s[ROWS:])
-        hides = [opening] * len(parts)
-        top = jnp.maximum(peak(parts, hides), stat[0, step, 0:1])
+        before = slot(jnp.maximum(g - 1, 0))
+        pvt[...] = sv[before].reshape(flat).T
+        prev_phase(sk[before].reshape(flat), None)
+
+    for e in range(Y):
+        coarse_to_mate(e).wait_recv()
+
+    coarse_count = G * B * N
+    cvt[...] = cc[1].T
+    k = lax.broadcasted_iota(jnp.int32, (coarse_count, ROWS), 0)
+    seen = ((k // N) % B) * G + k // (B * N) < position
+    bias[...] = jnp.where(seen, 0.0, -FAR)
+    kc, qc = iotas(N)
+    ends = kc * CMP_BLOCK + (CMP_BLOCK - 1) - qc
+
+    def coarse_front(step):
+        s = scores(cc[0, : coarse_count + N, :], qs[step])
+        parts = [
+            s[:coarse_count] + jnp.concatenate([bias[...]] * HEADS, axis=1),
+            jnp.where(ends <= step * ROWS, s[coarse_count:], -FAR),
+        ]
+        hides = [None] * len(parts)
+        return parts, hides, jnp.maximum(peak(parts, hides), 0.0)
+
+    def coarse_back(step, parts, hides, top):
         w, total = weigh(parts, hides, top)
-        mixed, total = join(0, step, times(pvt[:, low:], w), top, total, top)
-        acc[step] = acc[step] + mixed * (gate(2, step) / total)
+        w = jnp.concatenate([w, jnp.zeros((ROWS - N, LANES), BF16)], axis=0)
+        total = total + jnp.exp2(-top)
+        acc[step] = times(cvt[...], w) * (gate(0, step) / total)
+
+    pipeline(*spans(coarse_front, coarse_back))
+
+    @when(g == 0)
+    def _():
+        @when(b > 0)
+        def _():
+            for c in range(2):
+                for h in halves:
+                    to_next(c, h).wait_recv()
+
+        opening = jnp.where(b == 0, FAR, 0.0).astype(F32)
+        pvt[...] = pv[...].reshape(flat).T
+        prev_phase(pk[...].reshape(flat), opening)
 
     for c in range(2):
         for d in range(1, B):
@@ -527,33 +576,37 @@
         fk[pl.ds(i * SEL_BLOCK, SEL_BLOCK), :] = jnp.where(near, sk[rank], ik[owner])
         fvt[:, pl.ds(i * SEL_BLOCK, SEL_BLOCK)] = jnp.where(near, sv[rank], iv[owner]).T
 
-    def far_step(step, carry):
+    def far_front(step):
         parts, hides = fine_parts(step, near_count, TOPN)
         top = peak(parts, hides)
         if near_count > 0:
             top = jnp.maximum(top, stat[1, step, 0:1])
+        return parts, hides, top
+
+    def far_back(step, parts, hides, top):
         w, total = weigh(parts, hides, top)
         mixed = times(fvt[:, near_count * SEL_BLOCK :], w)
         if near_count > 0:
-            mixed, total = join(1, step, mixed, top, total, top)
-        mixed = acc[step] + mixed * (gate(1, step) / total)
+            mixed, total = join(1, step, mixed, total, top)
+        mixed = (acc[step] + part[0, step] + mixed * (gate(1, step) / total)).astype(BF16)
         for h in range(HEADS):
-            out[pl.ds(step * ROWS, ROWS), h * HEAD_DIM : (h + 1) * HEAD_DIM] = mixed[
+            out[step * ROWS : (step + 1) * ROWS, h * HEAD_DIM : (h + 1) * HEAD_DIM] = mixed[
                 :, h * ROWS : (h + 1) * ROWS
-            ].T.astype(BF16)
-        return carry
-
-    lax.fori_loop(0, STEPS, far_step, 0, unroll=True)
+            ].T
+
+    pipeline(*spans(far_front, far_back))
 
     for c in range(2):
-        for e in range(1, Y):
-            over_y(c, e).wait_send()
-        for e in range(Y):
-            to_mate(c, e).wait_send()
+        for h in halves:
+            for e in range(1, Y):
+                over_y(c, e, h).wait_send()
+            for e in range(Y):
+                to_mate(c, e, h).wait_send()
 
         @when(source)
         def _(c=c):
-            to_next(c).wait_send()
+            for h in halves:
+                to_next(c, h).wait_send()
 
         for d in range(1, B):
 
@@ -584,6 +637,7 @@
     STEPS = T // ROWS
     own_blocks = T // SEL_BLOCK
     inner, hidden = key_in.shape
+    near_keys = min(max(TOPN - (B - 1), 0), own_blocks) * SEL_BLOCK
     anywhere = pl.BlockSpec(memory_space=pl.ANY)
     dma = pltpu.SemaphoreType.DMA
     regular = pltpu.SemaphoreType.REGULAR
@@ -615,26 +669,27 @@
             blocks(B),
             blocks(B - 1),
             blocks(B - 1),
-            buf(G, 2, B * N, HEAD_DIM),
+            buf(2, G * B * N + ROWS, HEAD_DIM),
             buf(HEAD_DIM, G * B * N + ROWS),
-            buf(STEPS, LANES, 2 * HEAD_DIM),
+            buf(STEPS, 2 * HEAD_DIM, LANES),
             buf(HEAD_DIM, T),
             buf(HEAD_DIM, T),
             buf(TOPN * SEL_BLOCK, HEAD_DIM),
             buf(HEAD_DIM, TOPN * SEL_BLOCK),
             buf(G * B * N, ROWS, dtype=F32),
+            buf(STEPS, max(near_keys, SEL_BLOCK), LANES),
             buf(STEPS, HEAD_DIM, LANES, dtype=F32),
             buf(2, STEPS, HEAD_DIM, LANES, dtype=F32),
             buf(2, STEPS, 8, LANES, dtype=F32),
             buf(3 * HEADS, T, dtype=F32),
             dma((6,)),
             dma((4,)),
-            dma((2, Y)),
-            dma((2, Y)),
-            dma((2, Y)),
-            dma((2, Y)),
-            dma((2,)),
-            dma((2,)),
+            dma((2, Y, 2)),
+            dma((2, Y, 2)),
+            dma((2, Y, 2)),
+            dma((2, Y, 2)),
+            dma((2, 2)),
+            dma((2, 2)),
             dma((2, B)),
             dma((2, B)),
             dma((B,)),
@@ -642,7 +697,6 @@
             dma((2, Y)),
             dma((2, Y)),
             regular((B,)),
-            regular,
         ],
         compiler_params=pltpu.CompilerParams(
             collective_id=0, has_side_effects=True, vmem_limit_bytes=56 << 20

time: 25.8 us -> 21.1 us (0.82)
  the two profiles are of different devices: /device:TPU:17 before, /device:TPU:16 now
where the time goes in v2:
time: 21.1 us; the launch traced here: 21 us
  Pallas kernels  20.2 us (96%)
  local copies, waits for them, and re-layouts  0.8 us (4%)
    pallas_call x1, Pallas kernels, per_device(): pl.pallas_call(functools.partial(kernel, B, G), out_shape=pltpu.VMEM(quer...  20.2 us
    unnamed x1, local copies, waits for them, and re-layouts  0.8 us

profile of v2, /device:TPU:16, one launch (start us, length us, event | category | flops | bytes accessed | tf_op | source)
XLA Modules:
  0.0 21.0 jit_solution(2048074633276768997)
XLA Ops:
  0.0 20.2 %shard_map.100 = bf16[512,512]{1,0:T(8,128)(2,1)S(1)} custom-call(s32[16,32]{1,0:T(8,128)} %bitcast.7, bf16[512,512]{1,0:T(8,128)(2,1)} %queries_in.1, bf16[8,64,128]{2,1,0:T(8,128)(2,1)} %bitcast.4, bf16[8,64,128]{2,1,0:T(8,128)(2,1)} %bitcast.5, bf16[4096,256]{1,0:T(8,128)(2,1)} %key_in.1, bf16[256,128]{1,0:T(8,128)(2,1)} %key_out.1, ...), custom_call_target="tpu_custom_call" | custom-call | tf_op jit(solution)/shard_map/pallas_call | solution.py:651
  20.2 0.8 %copy.12 = bf16[512,512]{1,0:T(8,128)(2,1)} copy(bf16[512,512]{1,0:T(8,128)(2,1)S(1)} %shard_map.100) | data formatting | bytes 1048576

commit v3 on v2

--- a/solution.py
+++ b/solution.py
@@ -10,6 +10,7 @@
 
 HEAD_DIM = 128
 HEADS = 4
+TALL = HEAD_DIM + 16
 CMP_BLOCK = 32
 SEL_BLOCK = 64
 TOPN = 16
@@ -45,17 +46,16 @@
 
 
 def weigh(parts, hides, top):
-    packed, sums = [], []
+    packed = []
     for s, hide in zip(parts, hides):
         w = jnp.exp2(s - (top if hide is None else top + hide))
         packed.append(w.astype(BF16))
-        sums.append(jnp.sum(rows8(w), axis=0))
-    total = jnp.sum(functools.reduce(jnp.add, sums), axis=0, keepdims=True)
-    return jnp.concatenate(packed, axis=0), total
+    return jnp.concatenate(packed, axis=0)
 
 
 def times(vt, w):
-    return jnp.dot(vt, w, preferred_element_type=F32)
+    both = jnp.dot(vt, w, preferred_element_type=F32)
+    return both[:HEAD_DIM], both[HEAD_DIM : HEAD_DIM + 1]
 
 
 def pipeline(fronts, backs):
@@ -115,6 +115,7 @@
     stv,
     cc,
     cvt,
+    cvt_far,
     qs,
     wvt,
     pvt,
@@ -162,6 +163,8 @@
     staged = (stk, stv)
     inbox = (ik, iv)
 
+    flat = (T, HEAD_DIM)
+
     def slot(column):
         return pl.ds(column * own_blocks, own_blocks)
 
@@ -203,14 +206,14 @@
             )
         )
     ]
-    for load in own_load + [q_load, gate_load, shift_load, sel_load] + weight_loads:
+    for load in own_load + [q_load, shift_load] + weight_loads[0::2] + [gate_load, sel_load]:
         load.start()
 
     cc[...] = jnp.zeros_like(cc)
-    pk[...] = jnp.zeros_like(pk)
-    pv[...] = jnp.zeros_like(pv)
-
-    source = jnp.logical_and(g == 1, b < B - 1)
+
+    source = jnp.logical_and(g == G - 1, b < B - 1)
+    crossed = jnp.logical_and(g == 1, b < B - 1)
+    bridge = jnp.logical_and(g == G - 2, b > 0)
     barrier = pltpu.get_barrier_semaphore()
 
     def greet(dev):
@@ -223,6 +226,37 @@
         @when(b + d < B)
         def _(d=d):
             greet(at(b + d, g))
+
+    for load in own_load:
+        load.wait()
+    for load in weight_loads[1::2]:
+        load.start()
+    mine_rows = pl.ds(pl.multiple_of((g * B + b) * N, N), N)
+
+    def compress(c):
+        shift = positions[c].astype(F32)
+        tokens = row[c][slot(g)].reshape(flat).astype(F32).reshape(N, CMP_BLOCK, HEAD_DIM)
+        shifted[c] = (tokens + shift[None]).reshape(flat)
+        for load in weight_loads[c::2]:
+            load.wait()
+        wide = jnp.concatenate(
+            [shifted[c, pl.ds(t, N, stride=CMP_BLOCK), :].astype(BF16) for t in range(CMP_BLOCK)],
+            axis=1,
+        )
+        hidden = jax.nn.silu(jnp.dot(wide, w_in[c], preferred_element_type=F32)).astype(BF16)
+        mine = jnp.dot(hidden, w_out[c], preferred_element_type=F32).astype(BF16)
+        cc[c, mine_rows, :] = mine
+        cc[c, G * B * N : G * B * N + N, :] = mine
+
+    shift_load.wait()
+
+    early = jnp.logical_and(b == 0, y == 0)
+    late = jnp.logical_or(b > 0, y > 0)
+
+    @when(early)
+    def _():
+        compress(0)
+        compress(1)
 
     pl.semaphore_wait(barrier, G - 1 + b)
 
@@ -238,22 +272,20 @@
         piece = row[c].at[piece_of(((y - e + Y) % Y) * 2 + core, h)]
         return remote(piece, piece, m_s.at[c, e, h], m_r.at[c, e, h], at(b, mate))
 
-    def to_next(c, h):
-        return remote(
-            row[c].at[piece_of(G - 1, h)],
-            prev[c].at[piece_of(0, h)],
-            p_s.at[c, h],
-            p_r.at[c, h],
-            at((b + 1) % B, 0),
-        )
+    def keys_on():
+        return remote(sk.at[slot(G - 1)], pk, p_s.at[0], p_r.at[0], at((b + 1) % B, 0))
+
+    def values_on():
+        return remote(sv.at[slot(G - 1)], pv, p_s.at[1], p_r.at[1], at((b + 1) % B, G - 2))
+
+    def values_over():
+        return remote(pv, pv, p_s.at[2], p_r.at[2], at(b, 0))
 
     def block_out(c, d):
         return remote(
             staged[c].at[d - 1], inbox[c].at[b], b_s.at[c, d], b_r.at[c, d], at((b + d) % B, g)
         )
 
-    mine_rows = pl.ds(pl.multiple_of((g * B + b) * N, N), N)
-
     def column_rows(column):
         return pl.ds(pl.multiple_of(column * B * N, N), B * N)
 
@@ -271,12 +303,10 @@
         return remote(piece, piece, f_s.at[1, e], f_r.at[1, e], at(b, mate))
 
     halves = range(2)
-    own_load[0].wait()
     for h in halves:
         for e in range(1, Y):
             over_y(0, e, h).start()
         to_mate(0, 0, h).start()
-    own_load[1].wait()
     for h in halves:
         to_mate(1, 0, h).start()
 
@@ -295,37 +325,9 @@
             qs[step, :HEAD_DIM, h * ROWS : (h + 1) * ROWS] = high
             qs[step, HEAD_DIM:, h * ROWS : (h + 1) * ROWS] = (piece - high.astype(F32)).astype(BF16)
 
-    shift_load.wait()
-    flat = (T, HEAD_DIM)
-    for c in range(2):
-        shift = positions[c].astype(F32)
-        tokens = row[c][slot(g)].reshape(flat).astype(F32).reshape(N, CMP_BLOCK, HEAD_DIM)
-        shifted[c] = (tokens + shift[None]).reshape(flat)
-    wvt[...] = sv[slot(g)].reshape(flat).T
-    for load in weight_loads:
-        load.wait()
-    for c in range(2):
-        wide = jnp.concatenate(
-            [shifted[c, pl.ds(t, N, stride=CMP_BLOCK), :].astype(BF16) for t in range(CMP_BLOCK)],
-            axis=1,
-        )
-        hidden = jax.nn.silu(jnp.dot(wide, w_in[c], preferred_element_type=F32)).astype(BF16)
-        mine = jnp.dot(hidden, w_out[c], preferred_element_type=F32).astype(BF16)
-        cc[c, mine_rows, :] = mine
-        cc[c, G * B * N : G * B * N + N, :] = mine
-    for h in halves:
-        for e in range(1, Y):
-            over_y(1, e, h).start()
-
-    def coarse_on(low, high):
-        for d in range(low, high):
-
-            @when(b + d < B)
-            def _(d=d):
-                pl.semaphore_wait(ready.at[d], 1)
-                coarse_out(d).start()
-
-    coarse_on(1, B // 2)
+    for turned in (wvt, pvt, cvt, cvt_far, fvt):
+        turned[HEAD_DIM:, :] = jnp.ones_like(turned[HEAD_DIM:, :])
+    wvt[:HEAD_DIM] = sv[slot(g)].reshape(flat).T
 
     def iotas(count):
         k = lax.broadcasted_iota(jnp.int32, (count, LANES), 0)
@@ -338,50 +340,48 @@
             [gates[n * HEADS + h : n * HEADS + h + 1, cols] for h in range(HEADS)], axis=1
         )
 
-    def keep(which, step, mixed, top, total):
+    def keep(which, step, top, mixed, total):
         part[which, step] = mixed
         stat[which, step, 0:1] = top
         stat[which, step, 1:2] = total
 
-    def join(which, step, mixed, total, best):
+    def join(which, step, best, mixed, total):
         old = jnp.exp2(stat[which, step, 0:1] - best)
         return part[which, step] * old + mixed, stat[which, step, 1:2] * old + total
 
-    kd, qd = iotas(ROWS)
-    own_keys = sk[slot(g)].reshape(flat)
-
-    def own_front(step):
-        count = (step + 1) * ROWS
-        s = scores(own_keys[:count], qs[step])
-        parts = [jnp.where(kd <= qd, s[count - ROWS :], -FAR)]
-        if step > 0:
-            parts = [s[: count - ROWS]] + parts
-        hides = [None] * len(parts)
-        return parts, hides, peak(parts, hides)
-
-    def own_back(step, parts, hides, top):
-        w, total = weigh(parts, hides, top)
-        keep(0, step, times(wvt[:, : (step + 1) * ROWS], w), top, total)
-
-    def spans(front, back):
-        return (
-            [functools.partial(front, step) for step in range(STEPS)],
-            [functools.partial(back, step) for step in range(STEPS)],
-        )
-
-    pipeline(*spans(own_front, own_back))
-    coarse_on(B // 2, B)
-
-    def relay(c, h):
+    @when(late)
+    def _():
+        compress(0)
+
+    for h in halves:
         for e in range(1, Y):
-            over_y(c, e, h).wait_recv()
-            to_mate(c, e, h).start()
-
-        @when(source)
-        def _():
-            to_next(c, h).start()
-
-    relay(0, 0)
+            over_y(1, e, h).start()
+
+    @when(source)
+    def _():
+        pl.semaphore_wait(ready.at[1], 1)
+        values_on().start()
+
+    @when(late)
+    def _():
+        compress(1)
+
+    def coarse_on(low, high, which=True):
+        for d in range(low, high):
+
+            @when(jnp.logical_and(b + d < B, which))
+            def _(d=d):
+                if d == 1:
+
+                    @when(g < G - 1)
+                    def _():
+                        pl.semaphore_wait(ready.at[d], 1)
+                else:
+                    pl.semaphore_wait(ready.at[d], 1)
+                coarse_out(d).start()
+
+    coarse_on(1, B // 2, late)
+
     gate_load.wait()
     gates[...] = jax.nn.sigmoid(across(gate_weight[...], queries[...]))
     sel_load.wait()
@@ -420,8 +420,40 @@
         owner = jnp.where(near, 0, owner_of(code - per_row))
         return near, rank, owner, start
 
+    kd, qd = iotas(ROWS)
+    own_keys = sk[slot(g)].reshape(flat)
+
+    def own_front(step):
+        count = (step + 1) * ROWS
+        s = scores(own_keys[:count], qs[step])
+        parts = [jnp.where(kd <= qd, s[count - ROWS :], -FAR)]
+        if step > 0:
+            parts = [s[: count - ROWS]] + parts
+        hides = [None] * len(parts)
+        return parts, hides, peak(parts, hides)
+
+    def own_back(step, parts, hides, top):
+        w = weigh(parts, hides, top)
+        keep(0, step, top, *times(wvt[:, : (step + 1) * ROWS], w))
+
+    def spans(front, back):
+        return (
+            [functools.partial(front, step) for step in range(STEPS)],
+            [functools.partial(back, step) for step in range(STEPS)],
+        )
+
+    pipeline(*spans(own_front, own_back))
+    coarse_on(1, B // 2, early)
+    coarse_on(B // 2, B)
+
+    def relay(c, h):
+        for e in range(1, Y):
+            over_y(c, e, h).wait_recv()
+            to_mate(c, e, h).start()
+
+    relay(0, 0)
     def spread(c):
-        for e in range(Y):
+        for e in range(1, Y):
             for h in halves:
                 to_mate(c, e, h).wait_recv()
         for d in range(B - 1, 0, -1):
@@ -438,15 +470,49 @@
 
     relay(0, 1)
 
-    for d in range(1, B):
-
-        @when(b - d >= 0)
-        def _(d=d):
-            coarse_out(d).wait_recv()
-
-    for e in range(1, Y):
-        coarse_over_y(e).start()
-    coarse_to_mate(0).start()
+    @when(crossed)
+    def _():
+        keys_on().start()
+
+    for c in range(2):
+        for h in halves:
+            to_mate(c, 0, h).wait_recv()
+
+    def prev_phase(prev_keys):
+        def prev_front(step):
+            s = scores(prev_keys[step * ROWS :], qs[step])
+            parts = [jnp.where(kd > qd, s[:ROWS], -FAR)]
+            if step < STEPS - 1:
+                parts.append(s[ROWS:])
+            hides = [None] * len(parts)
+            return parts, hides, jnp.maximum(peak(parts, hides), stat[0, step, 0:1])
+
+        def prev_back(step, parts, hides, top):
+            w = weigh(parts, hides, top)
+            mixed, total = join(0, step, top, *times(pvt[:, step * ROWS :], w))
+            part[0, step] = mixed * (gate(2, step) / total)
+
+        pipeline(*spans(prev_front, prev_back))
+
+    def prev_before():
+        before = slot((g + G - 1) % G)
+        pvt[:HEAD_DIM] = sv[before].reshape(flat).T
+        prev_phase(sk[before].reshape(flat))
+
+    @when(core == 1)
+    def _():
+        prev_before()
+
+    def coarse_gather():
+        for d in range(1, B):
+
+            @when(b - d >= 0)
+            def _(d=d):
+                coarse_out(d).wait_recv()
+
+        for e in range(1, Y):
+            coarse_over_y(e).start()
+        coarse_to_mate(0).start()
 
     spread(0)
 
@@ -476,105 +542,179 @@
         return parts, hides, peak(parts, hides)
 
     def near_back(step, parts, hides, top):
-        w, total = weigh(parts, hides, top)
-        wnear[step] = w
+        wnear[step] = weigh(parts, hides, top)
         stat[1, step, 0:1] = top
-        stat[1, step, 1:2] = total
+
+    @when(core == 1)
+    def _():
+        relay(1, 0)
+        coarse_gather()
 
     half = STEPS // 2
     if near_count > 0:
         near_fronts, near_backs = spans(near_front, near_back)
         pipeline(near_fronts[:half], near_backs[:half])
-    relay(1, 0)
+    @when(core == 0)
+    def _():
+        relay(1, 0)
+        coarse_gather()
+
+    @when(bridge)
+    def _():
+        values_on().wait_recv()
+        values_over().start()
+
+    @when(core == 1)
+    def _():
+        relay(1, 1)
+
     if near_count > 0:
         pipeline(near_fronts[half:], near_backs[half:])
-    relay(1, 1)
+
+    chip = 2 * B * N
+
+    def chip_rows(e):
+        return pl.ds(pl.multiple_of(((y + e) % Y) * chip, chip), chip)
+
+    k = lax.broadcasted_iota(jnp.int32, (chip, ROWS), 0)
+    for e in range(Y):
+        column = ((y + e) % Y) * 2 + k // (B * N)
+        seen = (k % (B * N)) // N * G + column < position
+        bias[pl.ds(e * chip, chip), :] = jnp.where(seen, 0.0, -FAR)
+
+    def coarse_phase():
+        kc, qc = iotas(N)
+        ends = kc * CMP_BLOCK + (CMP_BLOCK - 1) - qc
+        mine = pl.ds(G * B * N, N)
+        coarse_to_mate(0).wait_recv()
+        cvt[:HEAD_DIM, :chip] = cc[1, chip_rows(0), :].T
+        cvt[:HEAD_DIM, chip:] = cc[1, pl.ds(G * B * N, ROWS), :].T
+
+        def coarse_front(step):
+            k = jnp.concatenate([cc[0, chip_rows(0), :], cc[0, mine, :]], axis=0)
+            s = scores(k, qs[step])
+            parts = [
+                s[:chip] + jnp.concatenate([bias[:chip, :]] * HEADS, axis=1),
+                jnp.where(ends <= step * ROWS, s[chip:], -FAR),
+            ]
+            hides = [None] * len(parts)
+            return parts, hides, jnp.maximum(peak(parts, hides), 0.0)
+
+        def coarse_back(step, parts, hides, top):
+            w = weigh(parts, hides, top)
+            w = jnp.concatenate([w, jnp.zeros((ROWS - N, LANES), BF16)], axis=0)
+            keep(2, step, top, *times(cvt[...], w))
+
+        return spans(coarse_front, coarse_back)
+
+    @when(core == 0)
+    def _():
+        relay(1, 1)
+        pipeline(*coarse_phase())
+
     spread(1)
 
     if near_count > 0:
         for i in range(near_count):
-            fvt[:, pl.ds(i * SEL_BLOCK, SEL_BLOCK)] = sv[entries[i][1]].T
+            fvt[:HEAD_DIM, pl.ds(i * SEL_BLOCK, SEL_BLOCK)] = sv[entries[i][1]].T
         for step in range(STEPS):
-            part[1, step] = times(fvt[:, : near_count * SEL_BLOCK], wnear[step])
+            mixed, total = times(fvt[:, : near_count * SEL_BLOCK], wnear[step])
+            part[1, step] = mixed
+            stat[1, step, 1:2] = total
+
+    def coarse_relay():
+        for e in range(1, Y):
+            coarse_over_y(e).wait_recv()
+            coarse_to_mate(e).start()
+
+    @when(core == 0)
+    def _():
+        coarse_relay()
+
+    @when(core == 1)
+    def _():
+        fronts, backs = coarse_phase()
+        pipeline(fronts[:half], backs[:half])
+        coarse_relay()
+        pipeline(fronts[half:], backs[half:])
+
+    @when(jnp.logical_and(core == 0, g > 0))
+    def _():
+        prev_before()
 
     for e in range(1, Y):
-        coarse_over_y(e).wait_recv()
-        coarse_to_mate(e).start()
-
-    def prev_phase(prev_keys, opening):
-        def prev_front(step):
-            s = scores(prev_keys[step * ROWS :], qs[step])
-            parts = [jnp.where(kd > qd, s[:ROWS], -FAR)]
-            if step < STEPS - 1:
-                parts.append(s[ROWS:])
-            hides = [opening] * len(parts)
-            return parts, hides, jnp.maximum(peak(parts, hides), stat[0, step, 0:1])
-
-        def prev_back(step, parts, hides, top):
-            w, total = weigh(parts, hides, top)
-            mixed = times(pvt[:, step * ROWS :], w)
-            mixed, total = join(0, step, mixed, total, top)
-            part[0, step] = mixed * (gate(2, step) / total)
-
-        pipeline(*spans(prev_front, prev_back))
-
-    @when(g > 0)
-    def _():
-        before = slot(jnp.maximum(g - 1, 0))
-        pvt[...] = sv[before].reshape(flat).T
-        prev_phase(sk[before].reshape(flat), None)
-
+        coarse_to_mate(e).wait_recv()
+
+    cvt_far[:HEAD_DIM] = jnp.concatenate([cc[1, chip_rows(e), :] for e in range(1, Y)], axis=0).T
+
+    def coarse_far_front(step):
+        k = jnp.concatenate([cc[0, chip_rows(e), :] for e in range(1, Y)], axis=0)
+        off = bias[pl.ds(chip, (Y - 1) * chip), :]
+        parts = [scores(k, qs[step]) + jnp.concatenate([off] * HEADS, axis=1)]
+        return parts, [None], jnp.maximum(peak(parts, [None]), stat[2, step, 0:1])
+
+    def coarse_far_back(step, parts, hides, top):
+        w = weigh(parts, hides, top)
+        mixed, total = join(2, step, top, *times(cvt_far[...], w))
+        acc[step] = mixed * (gate(0, step) / (total + jnp.exp2(-top)))
+
+    pipeline(*spans(coarse_far_front, coarse_far_back))
+
+    @when(jnp.logical_and(g == 0, b > 0))
+    def _():
+        keys_on().wait_recv()
+        values_over().wait_recv()
+        pvt[:HEAD_DIM] = pv[...].reshape(flat).T
+        prev_phase(pk[...].reshape(flat))
+
+    @when(position == 0)
+    def _():
+        for step in range(STEPS):
+            part[0, step] = part[0, step] * (gate(2, step) / stat[0, step, 1:2])
+
+    for c in range(2):
+        for h in halves:
+            for e in range(1, Y):
+                over_y(c, e, h).wait_send()
+            for e in range(Y):
+                to_mate(c, e, h).wait_send()
+
+    @when(source)
+    def _():
+        values_on().wait_send()
+
+    @when(crossed)
+    def _():
+        keys_on().wait_send()
+
+    @when(bridge)
+    def _():
+        values_over().wait_send()
+
+    for d in range(1, B):
+
+        @when(b + d < B)
+        def _(d=d):
+            coarse_out(d).wait_send()
+            for c in range(2):
+                block_out(c, d).wait_send()
+
+    for e in range(1, Y):
+        coarse_over_y(e).wait_send()
     for e in range(Y):
-        coarse_to_mate(e).wait_recv()
-
-    coarse_count = G * B * N
-    cvt[...] = cc[1].T
-    k = lax.broadcasted_iota(jnp.int32, (coarse_count, ROWS), 0)
-    seen = ((k // N) % B) * G + k // (B * N) < position
-    bias[...] = jnp.where(seen, 0.0, -FAR)
-    kc, qc = iotas(N)
-    ends = kc * CMP_BLOCK + (CMP_BLOCK - 1) - qc
-
-    def coarse_front(step):
-        s = scores(cc[0, : coarse_count + N, :], qs[step])
-        parts = [
-            s[:coarse_count] + jnp.concatenate([bias[...]] * HEADS, axis=1),
-            jnp.where(ends <= step * ROWS, s[coarse_count:], -FAR),
-        ]
-        hides = [None] * len(parts)
-        return parts, hides, jnp.maximum(peak(parts, hides), 0.0)
-
-    def coarse_back(step, parts, hides, top):
-        w, total = weigh(parts, hides, top)
-        w = jnp.concatenate([w, jnp.zeros((ROWS - N, LANES), BF16)], axis=0)
-        total = total + jnp.exp2(-top)
-        acc[step] = times(cvt[...], w) * (gate(0, step) / total)
-
-    pipeline(*spans(coarse_front, coarse_back))
-
-    @when(g == 0)
-    def _():
-        @when(b > 0)
-        def _():
+        coarse_to_mate(e).wait_send()
+
+    for d in range(1, B):
+
+        @when(b - d >= 0)
+        def _(d=d):
             for c in range(2):
-                for h in halves:
-                    to_next(c, h).wait_recv()
-
-        opening = jnp.where(b == 0, FAR, 0.0).astype(F32)
-        pvt[...] = pv[...].reshape(flat).T
-        prev_phase(pk[...].reshape(flat), opening)
-
-    for c in range(2):
-        for d in range(1, B):
-
-            @when(b - d >= 0)
-            def _(c=c, d=d):
                 block_out(c, d).wait_recv()
 
     for i in range(near_count, TOPN):
         near, rank, owner, _ = entries[i]
         fk[pl.ds(i * SEL_BLOCK, SEL_BLOCK), :] = jnp.where(near, sk[rank], ik[owner])
-        fvt[:, pl.ds(i * SEL_BLOCK, SEL_BLOCK)] = jnp.where(near, sv[rank], iv[owner]).T
+        fvt[:HEAD_DIM, pl.ds(i * SEL_BLOCK, SEL_BLOCK)] = jnp.where(near, sv[rank], iv[owner]).T
 
     def far_front(step):
         parts, hides = fine_parts(step, near_count, TOPN)
@@ -584,10 +724,10 @@
         return parts, hides, top
 
     def far_back(step, parts, hides, top):
-        w, total = weigh(parts, hides, top)
-        mixed = times(fvt[:, near_count * SEL_BLOCK :], w)
+        w = weigh(parts, hides, top)
+        mixed, total = times(fvt[:, near_count * SEL_BLOCK :], w)
         if near_count > 0:
-            mixed, total = join(1, step, mixed, total, top)
+            mixed, total = join(1, step, top, mixed, total)
         mixed = (acc[step] + part[0, step] + mixed * (gate(1, step) / total)).astype(BF16)
         for h in range(HEADS):
             out[step * ROWS : (step + 1) * ROWS, h * HEAD_DIM : (h + 1) * HEAD_DIM] = mixed[
@@ -595,35 +735,6 @@
             ].T
 
     pipeline(*spans(far_front, far_back))
-
-    for c in range(2):
-        for h in halves:
-            for e in range(1, Y):
-                over_y(c, e, h).wait_send()
-            for e in range(Y):
-                to_mate(c, e, h).wait_send()
-
-        @when(source)
-        def _(c=c):
-            for h in halves:
-                to_next(c, h).wait_send()
-
-        for d in range(1, B):
-
-            @when(b + d < B)
-            def _(c=c, d=d):
-                block_out(c, d).wait_send()
-
-    for d in range(1, B):
-
-        @when(b + d < B)
-        def _(d=d):
-            coarse_out(d).wait_send()
-
-    for e in range(1, Y):
-        coarse_over_y(e).wait_send()
-    for e in range(Y):
-        coarse_to_mate(e).wait_send()
 
 
 def per_device(
@@ -670,17 +781,18 @@
             blocks(B - 1),
             blocks(B - 1),
             buf(2, G * B * N + ROWS, HEAD_DIM),
-            buf(HEAD_DIM, G * B * N + ROWS),
+            buf(TALL, 2 * B * N + ROWS),
+            buf(TALL, (Y - 1) * 2 * B * N),
             buf(STEPS, 2 * HEAD_DIM, LANES),
-            buf(HEAD_DIM, T),
-            buf(HEAD_DIM, T),
+            buf(TALL, T),
+            buf(TALL, T),
             buf(TOPN * SEL_BLOCK, HEAD_DIM),
-            buf(HEAD_DIM, TOPN * SEL_BLOCK),
+            buf(TALL, TOPN * SEL_BLOCK),
             buf(G * B * N, ROWS, dtype=F32),
             buf(STEPS, max(near_keys, SEL_BLOCK), LANES),
             buf(STEPS, HEAD_DIM, LANES, dtype=F32),
-            buf(2, STEPS, HEAD_DIM, LANES, dtype=F32),
-            buf(2, STEPS, 8, LANES, dtype=F32),
+            buf(3, STEPS, HEAD_DIM, LANES, dtype=F32),
+            buf(3, STEPS, 8, LANES, dtype=F32),
             buf(3 * HEADS, T, dtype=F32),
             dma((6,)),
             dma((4,)),
@@ -688,8 +800,8 @@
             dma((2, Y, 2)),
             dma((2, Y, 2)),
             dma((2, Y, 2)),
-            dma((2, 2)),
-            dma((2, 2)),
+            dma((3,)),
+            dma((3,)),
             dma((2, B)),
             dma((2, B)),
             dma((B,)),

time: 21.1 us -> 19.3 us (0.915)
  the two profiles are of different devices: /device:TPU:16 before, /device:TPU:17 now
where the time goes in v3:
time: 19.3 us; the launch traced here: 19.1 us
  Pallas kernels  18.3 us (95%)
  local copies, waits for them, and re-layouts  0.8 us (4%)
    pallas_call x1, Pallas kernels, per_device(): pl.pallas_call(functools.partial(kernel, B, G), out_shape=pltpu.VMEM(quer...  18.3 us
    unnamed x1, local copies, waits for them, and re-layouts  0.8 us

profile of v3, /device:TPU:17, one launch (start us, length us, event | category | flops | bytes accessed | tf_op | source)
XLA Modules:
  0.0 19.1 jit_solution(10831379930554731863)
XLA Ops:
  0.0 18.3 %shard_map.100 = bf16[512,512]{1,0:T(8,128)(2,1)S(1)} custom-call(s32[16,32]{1,0:T(8,128)} %bitcast.7, bf16[512,512]{1,0:T(8,128)(2,1)} %queries_in.1, bf16[8,64,128]{2,1,0:T(8,128)(2,1)} %bitcast.4, bf16[8,64,128]{2,1,0:T(8,128)(2,1)} %bitcast.5, bf16[4096,256]{1,0:T(8,128)(2,1)} %key_in.1, bf16[256,128]{1,0:T(8,128)(2,1)} %key_out.1, ...), custom_call_target="tpu_custom_call" | custom-call | tf_op jit(solution)/shard_map/pallas_call | solution.py:762
  18.3 0.8 %copy.12 = bf16[512,512]{1,0:T(8,128)(2,1)} copy(bf16[512,512]{1,0:T(8,128)(2,1)S(1)} %shard_map.100) | data formatting | bytes 1048576

commit v4 on v3

--- a/solution.py
+++ b/solution.py
@@ -120,6 +120,7 @@
     wvt,
     pvt,
     fk,
+    fv,
     fvt,
     bias,
     wnear,
@@ -286,21 +287,31 @@
             staged[c].at[d - 1], inbox[c].at[b], b_s.at[c, d], b_r.at[c, d], at((b + d) % B, g)
         )
 
-    def column_rows(column):
-        return pl.ds(pl.multiple_of(column * B * N, N), B * N)
+    chunks = 4 if B % 4 == 0 else 1
+
+    def column_rows(column, k):
+        count = B // chunks * N
+        return pl.ds(pl.multiple_of(column * B * N + k * count, N), count)
+
+    def each_chunk(body):
+        for k in range(chunks):
+
+            @when(b >= k * (B // chunks))
+            def _(k=k):
+                body(k)
 
     def coarse_out(d):
         piece = cc.at[:, mine_rows, :]
         return remote(piece, piece, c_s.at[d], c_r.at[d], at((b + d) % B, g))
 
-    def coarse_over_y(e):
-        piece = cc.at[:, column_rows(g), :]
+    def coarse_over_y(e, k):
+        piece = cc.at[:, column_rows(g, k), :]
         dev = at(b, ((y + e) % Y) * 2 + core)
-        return remote(piece, piece, f_s.at[0, e], f_r.at[0, e], dev)
-
-    def coarse_to_mate(e):
-        piece = cc.at[:, column_rows(((y - e + Y) % Y) * 2 + core), :]
-        return remote(piece, piece, f_s.at[1, e], f_r.at[1, e], at(b, mate))
+        return remote(piece, piece, f_s.at[0, e, k], f_r.at[0, e, k], dev)
+
+    def coarse_to_mate(e, k):
+        piece = cc.at[:, column_rows(((y - e + Y) % Y) * 2 + core, k), :]
+        return remote(piece, piece, f_s.at[1, e, k], f_r.at[1, e, k], at(b, mate))
 
     halves = range(2)
     for h in halves:
@@ -353,18 +364,18 @@
     def _():
         compress(0)
 
+    @when(source)
+    def _():
+        pl.semaphore_wait(ready.at[1], 1)
+        values_on().start()
+
+    @when(late)
+    def _():
+        compress(1)
+
     for h in halves:
         for e in range(1, Y):
             over_y(1, e, h).start()
-
-    @when(source)
-    def _():
-        pl.semaphore_wait(ready.at[1], 1)
-        values_on().start()
-
-    @when(late)
-    def _():
-        compress(1)
 
     def coarse_on(low, high, which=True):
         for d in range(low, high):
@@ -456,13 +467,13 @@
         for e in range(1, Y):
             for h in halves:
                 to_mate(c, e, h).wait_recv()
-        for d in range(B - 1, 0, -1):
+        for d in range(1, B):
 
             @when(b + d < B)
             def _(d=d):
                 staged[c][d - 1] = row[c][picks[d - 1]]
 
-        for d in range(B - 1, 0, -1):
+        for d in range(1, B):
 
             @when(b + d < B)
             def _(d=d):
@@ -478,21 +489,37 @@
         for h in halves:
             to_mate(c, 0, h).wait_recv()
 
+    def prev_front(prev_keys, step):
+        s = scores(prev_keys[step * ROWS :], qs[step])
+        parts = [jnp.where(kd > qd, s[:ROWS], -FAR)]
+        if step < STEPS - 1:
+            parts.append(s[ROWS:])
+        hides = [None] * len(parts)
+        return parts, hides, jnp.maximum(peak(parts, hides), stat[0, step, 0:1])
+
     def prev_phase(prev_keys):
-        def prev_front(step):
-            s = scores(prev_keys[step * ROWS :], qs[step])
-            parts = [jnp.where(kd > qd, s[:ROWS], -FAR)]
-            if step < STEPS - 1:
-                parts.append(s[ROWS:])
-            hides = [None] * len(parts)
-            return parts, hides, jnp.maximum(peak(parts, hides), stat[0, step, 0:1])
-
-        def prev_back(step, parts, hides, top):
+        def back(step, parts, hides, top):
             w = weigh(parts, hides, top)
             mixed, total = join(0, step, top, *times(pvt[:, step * ROWS :], w))
             part[0, step] = mixed * (gate(2, step) / total)
 
-        pipeline(*spans(prev_front, prev_back))
+        fronts = [functools.partial(prev_front, prev_keys, step) for step in range(STEPS)]
+        pipeline(fronts, [functools.partial(back, step) for step in range(STEPS)])
+
+    def prev_weights(prev_keys):
+        fronts = [functools.partial(prev_front, prev_keys, step) for step in range(STEPS)]
+
+        def back(step, parts, hides, top):
+            wnear[step, : T - step * ROWS] = weigh(parts, hides, top)
+            stat[0, step, 2:3] = top
+
+        pipeline(fronts, [functools.partial(back, step) for step in range(STEPS)])
+
+    def prev_product():
+        for step in range(STEPS):
+            both = times(pvt[:, step * ROWS :], wnear[step, : T - step * ROWS])
+            mixed, total = join(0, step, stat[0, step, 2:3], *both)
+            part[0, step] = mixed * (gate(2, step) / total)
 
     def prev_before():
         before = slot((g + G - 1) % G)
@@ -510,9 +537,12 @@
             def _(d=d):
                 coarse_out(d).wait_recv()
 
-        for e in range(1, Y):
-            coarse_over_y(e).start()
-        coarse_to_mate(0).start()
+        def send(k):
+            for e in range(1, Y):
+                coarse_over_y(e, k).start()
+            coarse_to_mate(0, k).start()
+
+        each_chunk(send)
 
     spread(0)
 
@@ -542,7 +572,7 @@
         return parts, hides, peak(parts, hides)
 
     def near_back(step, parts, hides, top):
-        wnear[step] = weigh(parts, hides, top)
+        wnear[step, : near_count * SEL_BLOCK] = weigh(parts, hides, top)
         stat[1, step, 0:1] = top
 
     @when(core == 1)
@@ -586,7 +616,7 @@
         kc, qc = iotas(N)
         ends = kc * CMP_BLOCK + (CMP_BLOCK - 1) - qc
         mine = pl.ds(G * B * N, N)
-        coarse_to_mate(0).wait_recv()
+        each_chunk(lambda k: coarse_to_mate(0, k).wait_recv())
         cvt[:HEAD_DIM, :chip] = cc[1, chip_rows(0), :].T
         cvt[:HEAD_DIM, chip:] = cc[1, pl.ds(G * B * N, ROWS), :].T
 
@@ -615,35 +645,48 @@
     spread(1)
 
     if near_count > 0:
+        near_keys = near_count * SEL_BLOCK
         for i in range(near_count):
-            fvt[:HEAD_DIM, pl.ds(i * SEL_BLOCK, SEL_BLOCK)] = sv[entries[i][1]].T
+            fv[pl.ds(i * SEL_BLOCK, SEL_BLOCK), :] = sv[entries[i][1]]
+        fvt[:HEAD_DIM, :near_keys] = fv[:near_keys, :].T
         for step in range(STEPS):
-            mixed, total = times(fvt[:, : near_count * SEL_BLOCK], wnear[step])
+            mixed, total = times(
+                fvt[:, : near_count * SEL_BLOCK], wnear[step, : near_count * SEL_BLOCK]
+            )
             part[1, step] = mixed
             stat[1, step, 1:2] = total
 
     def coarse_relay():
+        def pass_on(k):
+            for e in range(1, Y):
+                coarse_over_y(e, k).wait_recv()
+                coarse_to_mate(e, k).start()
+
+        each_chunk(pass_on)
+
+    @when(core == 0)
+    def _():
+        coarse_relay()
+
+    @when(jnp.logical_and(g == 0, b > 0))
+    def _():
+        keys_on().wait_recv()
+        prev_weights(pk[...].reshape(flat))
+
+    @when(core == 1)
+    def _():
+        coarse_relay()
+        pipeline(*coarse_phase())
+
+    @when(jnp.logical_and(core == 0, g > 0))
+    def _():
+        prev_before()
+
+    def others_in(k):
         for e in range(1, Y):
-            coarse_over_y(e).wait_recv()
-            coarse_to_mate(e).start()
-
-    @when(core == 0)
-    def _():
-        coarse_relay()
-
-    @when(core == 1)
-    def _():
-        fronts, backs = coarse_phase()
-        pipeline(fronts[:half], backs[:half])
-        coarse_relay()
-        pipeline(fronts[half:], backs[half:])
-
-    @when(jnp.logical_and(core == 0, g > 0))
-    def _():
-        prev_before()
-
-    for e in range(1, Y):
-        coarse_to_mate(e).wait_recv()
+            coarse_to_mate(e, k).wait_recv()
+
+    each_chunk(others_in)
 
     cvt_far[:HEAD_DIM] = jnp.concatenate([cc[1, chip_rows(e), :] for e in range(1, Y)], axis=0).T
 
@@ -662,10 +705,9 @@
 
     @when(jnp.logical_and(g == 0, b > 0))
     def _():
-        keys_on().wait_recv()
         values_over().wait_recv()
         pvt[:HEAD_DIM] = pv[...].reshape(flat).T
-        prev_phase(pk[...].reshape(flat))
+        prev_product()
 
     @when(position == 0)
     def _():
@@ -699,10 +741,13 @@
             for c in range(2):
                 block_out(c, d).wait_send()
 
-    for e in range(1, Y):
-        coarse_over_y(e).wait_send()
-    for e in range(Y):
-        coarse_to_mate(e).wait_send()
+    def coarse_left(k):
+        for e in range(1, Y):
+            coarse_over_y(e, k).wait_send()
+        for e in range(Y):
+            coarse_to_mate(e, k).wait_send()
+
+    each_chunk(coarse_left)
 
     for d in range(1, B):
 
@@ -714,7 +759,8 @@
     for i in range(near_count, TOPN):
         near, rank, owner, _ = entries[i]
         fk[pl.ds(i * SEL_BLOCK, SEL_BLOCK), :] = jnp.where(near, sk[rank], ik[owner])
-        fvt[:HEAD_DIM, pl.ds(i * SEL_BLOCK, SEL_BLOCK)] = jnp.where(near, sv[rank], iv[owner]).T
+        fv[pl.ds(i * SEL_BLOCK, SEL_BLOCK), :] = jnp.where(near, sv[rank], iv[owner])
+    fvt[:HEAD_DIM, near_count * SEL_BLOCK :] = fv[near_count * SEL_BLOCK :, :].T
 
     def far_front(step):
         parts, hides = fine_parts(step, near_count, TOPN)
@@ -787,9 +833,10 @@
             buf(TALL, T),
             buf(TALL, T),
             buf(TOPN * SEL_BLOCK, HEAD_DIM),
+            buf(TOPN * SEL_BLOCK, HEAD_DIM),
             buf(TALL, TOPN * SEL_BLOCK),
             buf(G * B * N, ROWS, dtype=F32),
-            buf(STEPS, max(near_keys, SEL_BLOCK), LANES),
+            buf(STEPS, max(near_keys, T), LANES),
             buf(STEPS, HEAD_DIM, LANES, dtype=F32),
             buf(3, STEPS, HEAD_DIM, LANES, dtype=F32),
             buf(3, STEPS, 8, LANES, dtype=F32),
@@ -806,8 +853,8 @@
             dma((2, B)),
             dma((B,)),
             dma((B,)),
-            dma((2, Y)),
-            dma((2, Y)),
+            dma((2, Y, 4)),
+            dma((2, Y, 4)),
             regular((B,)),
         ],
         compiler_params=pltpu.CompilerParams(

time: 19.3 us -> 18.9 us (0.979)
  the two profiles are of different devices: /device:TPU:17 before, /device:TPU:24 now
where the time goes in v4:
time: 18.9 us; the launch traced here: 18.7 us
  Pallas kernels  17.9 us (95%)
  local copies, waits for them, and re-layouts  0.8 us (4%)
    pallas_call x1, Pallas kernels, per_device(): pl.pallas_call(functools.partial(kernel, B, G), out_shape=pltpu.VMEM(quer...  17.9 us
    unnamed x1, local copies, waits for them, and re-layouts  0.8 us

profile of v4, /device:TPU:24, one launch (start us, length us, event | category | flops | bytes accessed | tf_op | source)
XLA Modules:
  0.0 18.7 jit_solution(536779825752189372)
XLA Ops:
  0.0 17.9 %shard_map.100 = bf16[512,512]{1,0:T(8,128)(2,1)S(1)} custom-call(s32[16,32]{1,0:T(8,128)} %bitcast.7, bf16[512,512]{1,0:T(8,128)(2,1)} %queries_in.1, bf16[8,64,128]{2,1,0:T(8,128)(2,1)} %bitcast.4, bf16[8,64,128]{2,1,0:T(8,128)(2,1)} %bitcast.5, bf16[4096,256]{1,0:T(8,128)(2,1)} %key_in.1, bf16[256,128]{1,0:T(8,128)(2,1)} %key_out.1, ...), custom_call_target="tpu_custom_call" | custom-call | tf_op jit(solution)/shard_map/pallas_call | solution.py:808
  17.9 0.8 %copy.12 = bf16[512,512]{1,0:T(8,128)(2,1)} copy(bf16[512,512]{1,0:T(8,128)(2,1)S(1)} %shard_map.100) | data formatting | bytes 1048576

commit v5 on v4

--- a/solution.py
+++ b/solution.py
@@ -138,7 +138,6 @@
     p_r,
     b_s,
     b_r,
-    c_s,
     c_r,
     f_s,
     f_r,
@@ -207,31 +206,34 @@
             )
         )
     ]
-    for load in own_load + [q_load, shift_load] + weight_loads[0::2] + [gate_load, sel_load]:
+    for load in own_load:
         load.start()
-
     cc[...] = jnp.zeros_like(cc)
+    barrier = pltpu.get_barrier_semaphore()
+
+    def greet(dev):
+        pl.semaphore_signal(barrier, inc=1, device_id=dev, device_id_type=MESH)
+
+    for e in range(1, G):
+        greet(at(b, (g + e) % G))
+    for d in range(1, B):
+
+        @when(b + d < B)
+        def _(d=d):
+            greet(at(b + d, g))
+
+    for load in [q_load, shift_load] + weight_loads[0::2] + [gate_load, sel_load]:
+        load.start()
+
 
     source = jnp.logical_and(g == G - 1, b < B - 1)
     crossed = jnp.logical_and(g == 1, b < B - 1)
     bridge = jnp.logical_and(g == G - 2, b > 0)
-    barrier = pltpu.get_barrier_semaphore()
-
-    def greet(dev):
-        pl.semaphore_signal(barrier, inc=1, device_id=dev, device_id_type=MESH)
-
-    for e in range(1, G):
-        greet(at(b, (g + e) % G))
-    for d in range(1, B):
-
-        @when(b + d < B)
-        def _(d=d):
-            greet(at(b + d, g))
-
     for load in own_load:
         load.wait()
     for load in weight_loads[1::2]:
         load.start()
+
     mine_rows = pl.ds(pl.multiple_of((g * B + b) * N, N), N)
 
     def compress(c):
@@ -267,11 +269,11 @@
     def over_y(c, e, h):
         piece = row[c].at[piece_of(g, h)]
         dev = at(b, ((y + e) % Y) * 2 + core)
-        return remote(piece, piece, a_s.at[c, e, h], a_r.at[c, e, h], dev)
+        return remote(piece, piece, a_s.at[0], a_r.at[c, e - 1, h], dev)
 
     def to_mate(c, e, h):
         piece = row[c].at[piece_of(((y - e + Y) % Y) * 2 + core, h)]
-        return remote(piece, piece, m_s.at[c, e, h], m_r.at[c, e, h], at(b, mate))
+        return remote(piece, piece, m_s.at[0], m_r.at[c if e else 0, e], at(b, mate))
 
     def keys_on():
         return remote(sk.at[slot(G - 1)], pk, p_s.at[0], p_r.at[0], at((b + 1) % B, 0))
@@ -284,10 +286,11 @@
 
     def block_out(c, d):
         return remote(
-            staged[c].at[d - 1], inbox[c].at[b], b_s.at[c, d], b_r.at[c, d], at((b + d) % B, g)
+            staged[c].at[d - 1], inbox[c].at[b], b_s.at[d - 1], b_r.at[d - 1], at((b + d) % B, g)
         )
 
     chunks = 4 if B % 4 == 0 else 1
+    reach = B // chunks
 
     def column_rows(column, k):
         count = B // chunks * N
@@ -302,16 +305,19 @@
 
     def coarse_out(d):
         piece = cc.at[:, mine_rows, :]
-        return remote(piece, piece, c_s.at[d], c_r.at[d], at((b + d) % B, g))
+        return remote(piece, piece, b_s.at[d - 1], c_r.at[d - 1], at((b + d) % B, g))
 
     def coarse_over_y(e, k):
         piece = cc.at[:, column_rows(g, k), :]
         dev = at(b, ((y + e) % Y) * 2 + core)
-        return remote(piece, piece, f_s.at[0, e, k], f_r.at[0, e, k], dev)
+        return remote(piece, piece, f_s.at[k], f_r.at[e - 1, k], dev)
 
     def coarse_to_mate(e, k):
         piece = cc.at[:, column_rows(((y - e + Y) % Y) * 2 + core, k), :]
-        return remote(piece, piece, f_s.at[1, e, k], f_r.at[1, e, k], at(b, mate))
+        return remote(piece, piece, f_s.at[k], f_r.at[Y - 1 + e, k], at(b, mate))
+
+    def all_of(ref, sem):
+        return local(ref, ref, sem)
 
     halves = range(2)
     for h in halves:
@@ -325,7 +331,7 @@
 
         @when(b - d >= 0)
         def _(d=d):
-            pl.semaphore_signal(ready.at[d], inc=1, device_id=at(b - d, g), device_id_type=MESH)
+            pl.semaphore_signal(ready.at[d - 1], inc=1, device_id=at(b - d, g), device_id_type=MESH)
 
     q_load.wait()
     for step in range(STEPS):
@@ -366,12 +372,30 @@
 
     @when(source)
     def _():
-        pl.semaphore_wait(ready.at[1], 1)
+        pl.semaphore_wait(ready.at[0], 1)
         values_on().start()
 
     @when(late)
     def _():
         compress(1)
+
+    def coarse_gather():
+        for d in range(1, B):
+
+            @when(b - d >= 0)
+            def _(d=d):
+                coarse_out(d).wait_recv()
+
+        def send(k):
+            for e in range(1, Y):
+                coarse_over_y(e, k).start()
+            coarse_to_mate(0, k).start()
+
+        each_chunk(send)
+
+    @when(b == 0)
+    def _():
+        coarse_gather()
 
     for h in halves:
         for e in range(1, Y):
@@ -386,9 +410,9 @@
 
                     @when(g < G - 1)
                     def _():
-                        pl.semaphore_wait(ready.at[d], 1)
+                        pl.semaphore_wait(ready.at[d - 1], 1)
                 else:
-                    pl.semaphore_wait(ready.at[d], 1)
+                    pl.semaphore_wait(ready.at[d - 1], 1)
                 coarse_out(d).start()
 
     coarse_on(1, B // 2, late)
@@ -465,8 +489,7 @@
     relay(0, 0)
     def spread(c):
         for e in range(1, Y):
-            for h in halves:
-                to_mate(c, e, h).wait_recv()
+            all_of(sk.at[pl.ds(0, own_blocks)], m_r.at[c, e]).wait()
         for d in range(1, B):
 
             @when(b + d < B)
@@ -485,9 +508,7 @@
     def _():
         keys_on().start()
 
-    for c in range(2):
-        for h in halves:
-            to_mate(c, 0, h).wait_recv()
+    all_of(sk.at[pl.ds(0, 2 * own_blocks)], m_r.at[0, 0]).wait()
 
     def prev_front(prev_keys, step):
         s = scores(prev_keys[step * ROWS :], qs[step])
@@ -529,20 +550,6 @@
     @when(core == 1)
     def _():
         prev_before()
-
-    def coarse_gather():
-        for d in range(1, B):
-
-            @when(b - d >= 0)
-            def _(d=d):
-                coarse_out(d).wait_recv()
-
-        def send(k):
-            for e in range(1, Y):
-                coarse_over_y(e, k).start()
-            coarse_to_mate(0, k).start()
-
-        each_chunk(send)
 
     spread(0)
 
@@ -578,7 +585,11 @@
     @when(core == 1)
     def _():
         relay(1, 0)
-        coarse_gather()
+
+        @when(b > 0)
+        def _():
+            coarse_gather()
+
 
     half = STEPS // 2
     if near_count > 0:
@@ -587,7 +598,11 @@
     @when(core == 0)
     def _():
         relay(1, 0)
-        coarse_gather()
+
+        @when(b > 0)
+        def _():
+            coarse_gather()
+
 
     @when(bridge)
     def _():
@@ -714,12 +729,8 @@
         for step in range(STEPS):
             part[0, step] = part[0, step] * (gate(2, step) / stat[0, step, 1:2])
 
-    for c in range(2):
-        for h in halves:
-            for e in range(1, Y):
-                over_y(c, e, h).wait_send()
-            for e in range(Y):
-                to_mate(c, e, h).wait_send()
+    all_of(sk.at[pl.ds(0, (Y - 1) * 2 * own_blocks)], a_s.at[0]).wait()
+    all_of(sk, m_s.at[0]).wait()
 
     @when(source)
     def _():
@@ -737,15 +748,10 @@
 
         @when(b + d < B)
         def _(d=d):
-            coarse_out(d).wait_send()
-            for c in range(2):
-                block_out(c, d).wait_send()
+            all_of(cc.at[0, pl.ds(0, 2 * (N + SEL_BLOCK)), :], b_s.at[d - 1]).wait()
 
     def coarse_left(k):
-        for e in range(1, Y):
-            coarse_over_y(e, k).wait_send()
-        for e in range(Y):
-            coarse_to_mate(e, k).wait_send()
+        all_of(cc.at[0, pl.ds(0, (2 * Y - 1) * 2 * reach * N), :], f_s.at[k]).wait()
 
     each_chunk(coarse_left)
 
@@ -753,8 +759,7 @@
 
         @when(b - d >= 0)
         def _(d=d):
-            for c in range(2):
-                block_out(c, d).wait_recv()
+            all_of(sk.at[pl.ds(0, 2)], b_r.at[d - 1]).wait()
 
     for i in range(near_count, TOPN):
         near, rank, owner, _ = entries[i]
@@ -843,19 +848,18 @@
             buf(3 * HEADS, T, dtype=F32),
             dma((6,)),
             dma((4,)),
-            dma((2, Y, 2)),
-            dma((2, Y, 2)),
-            dma((2, Y, 2)),
-            dma((2, Y, 2)),
+            dma((1,)),
+            dma((2, Y - 1, 2)),
+            dma((1,)),
+            dma((2, Y)),
             dma((3,)),
             dma((3,)),
-            dma((2, B)),
-            dma((2, B)),
-            dma((B,)),
-            dma((B,)),
-            dma((2, Y, 4)),
-            dma((2, Y, 4)),
-            regular((B,)),
+            dma((B - 1,)),
+            dma((B - 1,)),
+            dma((B - 1,)),
+            dma((4,)),
+            dma((2 * Y - 1, 4)),
+            regular((B - 1,)),
         ],
         compiler_params=pltpu.CompilerParams(
             collective_id=0, has_side_effects=True, vmem_limit_bytes=56 << 20

time: 18.9 us -> 18.3 us (0.968)
  Pallas kernels: 17.9 us -> 17.3 us
    pallas_call x1, Pallas kernels: 17.9 us -> 17.3 us  [per_device(): pl.pallas_call(functools.partial(kernel, B, G), out_shape=pltpu.VMEM(quer...]
where the time goes in v5:
time: 18.3 us; the launch traced here: 18.1 us
  Pallas kernels  17.3 us (95%)
  local copies, waits for them, and re-layouts  0.8 us (4%)
    pallas_call x1, Pallas kernels, per_device(): pl.pallas_call(functools.partial(kernel, B, G), out_shape=pltpu.VMEM(quer...  17.3 us
    unnamed x1, local copies, waits for them, and re-layouts  0.8 us

profile of v5, /device:TPU:24, one launch (start us, length us, event | category | flops | bytes accessed | tf_op | source)
XLA Modules:
  0.0 18.1 jit_solution(1269069689650486725)
XLA Ops:
  0.0 17.3 %shard_map.100 = bf16[512,512]{1,0:T(8,128)(2,1)S(1)} custom-call(s32[16,32]{1,0:T(8,128)} %bitcast.7, bf16[512,512]{1,0:T(8,128)(2,1)} %queries_in.1, bf16[8,64,128]{2,1,0:T(8,128)(2,1)} %bitcast.4, bf16[8,64,128]{2,1,0:T(8,128)(2,1)} %bitcast.5, bf16[4096,256]{1,0:T(8,128)(2,1)} %key_in.1, bf16[256,128]{1,0:T(8,128)(2,1)} %key_out.1, ...), custom_call_target="tpu_custom_call" | custom-call | tf_op jit(solution)/shard_map/pallas_call | solution.py:813
  17.3 0.8 %copy.12 = bf16[512,512]{1,0:T(8,128)(2,1)} copy(bf16[512,512]{1,0:T(8,128)(2,1)S(1)} %shard_map.100) | data formatting | bytes 1048576

commit v6 on v5

--- a/solution.py
+++ b/solution.py
@@ -286,7 +286,7 @@
 
     def block_out(c, d):
         return remote(
-            staged[c].at[d - 1], inbox[c].at[b], b_s.at[d - 1], b_r.at[d - 1], at((b + d) % B, g)
+            staged[c].at[d - 1], inbox[c].at[b], b_s.at[0], b_r.at[0], at((b + d) % B, g)
         )
 
     chunks = 4 if B % 4 == 0 else 1
@@ -305,20 +305,30 @@
 
     def coarse_out(d):
         piece = cc.at[:, mine_rows, :]
-        return remote(piece, piece, b_s.at[d - 1], c_r.at[d - 1], at((b + d) % B, g))
+        return remote(piece, piece, b_s.at[0], c_r.at[0], at((b + d) % B, g))
 
     def coarse_over_y(e, k):
         piece = cc.at[:, column_rows(g, k), :]
         dev = at(b, ((y + e) % Y) * 2 + core)
-        return remote(piece, piece, f_s.at[k], f_r.at[e - 1, k], dev)
+        return remote(piece, piece, f_s.at[0], f_r.at[e - 1], dev)
 
     def coarse_to_mate(e, k):
         piece = cc.at[:, column_rows(((y - e + Y) % Y) * 2 + core, k), :]
-        return remote(piece, piece, f_s.at[k], f_r.at[Y - 1 + e, k], at(b, mate))
+        return remote(piece, piece, f_s.at[0], f_r.at[Y - 1 + e], at(b, mate))
 
     def all_of(ref, sem):
         return local(ref, ref, sem)
 
+    def counted(number, low, high, rows, sem):
+        for n in range(low, high):
+
+            @when(number == n)
+            def _(n=n):
+                all_of(w_in.at[0, pl.ds(0, n * rows), :], sem).wait()
+
+    coarse_bytes = N
+    chunk_bytes = reach * N
+    block_bytes = SEL_BLOCK
     halves = range(2)
     for h in halves:
         for e in range(1, Y):
@@ -380,11 +390,7 @@
         compress(1)
 
     def coarse_gather():
-        for d in range(1, B):
-
-            @when(b - d >= 0)
-            def _(d=d):
-                coarse_out(d).wait_recv()
+        counted(b, 1, B, coarse_bytes, c_r.at[0])
 
         def send(k):
             for e in range(1, Y):
@@ -631,7 +637,7 @@
         kc, qc = iotas(N)
         ends = kc * CMP_BLOCK + (CMP_BLOCK - 1) - qc
         mine = pl.ds(G * B * N, N)
-        each_chunk(lambda k: coarse_to_mate(0, k).wait_recv())
+        counted(b // reach + 1, 1, chunks + 1, chunk_bytes, f_r.at[Y - 1])
         cvt[:HEAD_DIM, :chip] = cc[1, chip_rows(0), :].T
         cvt[:HEAD_DIM, chip:] = cc[1, pl.ds(G * B * N, ROWS), :].T
 
@@ -672,9 +678,11 @@
             stat[1, step, 1:2] = total
 
     def coarse_relay():
+        for e in range(1, Y):
+            counted(b // reach + 1, 1, chunks + 1, chunk_bytes, f_r.at[e - 1])
+
         def pass_on(k):
             for e in range(1, Y):
-                coarse_over_y(e, k).wait_recv()
                 coarse_to_mate(e, k).start()
 
         each_chunk(pass_on)
@@ -697,11 +705,8 @@
     def _():
         prev_before()
 
-    def others_in(k):
-        for e in range(1, Y):
-            coarse_to_mate(e, k).wait_recv()
-
-    each_chunk(others_in)
+    for e in range(1, Y):
+        counted(b // reach + 1, 1, chunks + 1, chunk_bytes, f_r.at[Y - 1 + e])
 
     cvt_far[:HEAD_DIM] = jnp.concatenate([cc[1, chip_rows(e), :] for e in range(1, Y)], axis=0).T
 
@@ -744,22 +749,10 @@
     def _():
         values_over().wait_send()
 
-    for d in range(1, B):
-
-        @when(b + d < B)
-        def _(d=d):
-            all_of(cc.at[0, pl.ds(0, 2 * (N + SEL_BLOCK)), :], b_s.at[d - 1]).wait()
-
-    def coarse_left(k):
-        all_of(cc.at[0, pl.ds(0, (2 * Y - 1) * 2 * reach * N), :], f_s.at[k]).wait()
-
-    each_chunk(coarse_left)
-
-    for d in range(1, B):
-
-        @when(b - d >= 0)
-        def _(d=d):
-            all_of(sk.at[pl.ds(0, 2)], b_r.at[d - 1]).wait()
+    counted(B - 1 - b, 1, B, coarse_bytes + block_bytes, b_s.at[0])
+    counted(b // reach + 1, 1, chunks + 1, (2 * Y - 1) * chunk_bytes, f_s.at[0])
+
+    counted(b, 1, B, block_bytes, b_r.at[0])
 
     for i in range(near_count, TOPN):
         near, rank, owner, _ = entries[i]
@@ -854,11 +847,11 @@
             dma((2, Y)),
             dma((3,)),
             dma((3,)),
-            dma((B - 1,)),
-            dma((B - 1,)),
-            dma((B - 1,)),
-            dma((4,)),
-            dma((2 * Y - 1, 4)),
+            dma((1,)),
+            dma((1,)),
+            dma((1,)),
+            dma((1,)),
+            dma((2 * Y - 1,)),
             regular((B - 1,)),
         ],
         compiler_params=pltpu.CompilerParams(

time: 18.3 us -> 18 us (0.984)
  Pallas kernels: 17.3 us -> 17 us
    pallas_call x1, Pallas kernels: 17.3 us -> 17 us  [per_device(): pl.pallas_call(functools.partial(kernel, B, G), out_shape=pltpu.VMEM(quer...]
where the time goes in v6:
time: 18 us; the launch traced here: 17.8 us
  Pallas kernels  17 us (94%)
  local copies, waits for them, and re-layouts  0.8 us (4%)
    pallas_call x1, Pallas kernels, per_device(): pl.pallas_call(functools.partial(kernel, B, G), out_shape=pltpu.VMEM(quer...  17 us
    unnamed x1, local copies, waits for them, and re-layouts  0.8 us

profile of v6, /device:TPU:24, one launch (start us, length us, event | category | flops | bytes accessed | tf_op | source)
XLA Modules:
  0.0 17.8 jit_solution(14671328887948697346)
XLA Ops:
  0.0 17.0 %shard_map.100 = bf16[512,512]{1,0:T(8,128)(2,1)S(1)} custom-call(s32[16,32]{1,0:T(8,128)} %bitcast.7, bf16[512,512]{1,0:T(8,128)(2,1)} %queries_in.1, bf16[8,64,128]{2,1,0:T(8,128)(2,1)} %bitcast.4, bf16[8,64,128]{2,1,0:T(8,128)(2,1)} %bitcast.5, bf16[4096,256]{1,0:T(8,128)(2,1)} %key_in.1, bf16[256,128]{1,0:T(8,128)(2,1)} %key_out.1, ...), custom_call_target="tpu_custom_call" | custom-call | tf_op jit(solution)/shard_map/pallas_call | solution.py:806
  17.1 0.8 %copy.12 = bf16[512,512]{1,0:T(8,128)(2,1)} copy(bf16[512,512]{1,0:T(8,128)(2,1)S(1)} %shard_map.100) | data formatting | bytes 1048576

commit v7 on v6

--- a/solution.py
+++ b/solution.py
@@ -273,16 +273,16 @@
 
     def to_mate(c, e, h):
         piece = row[c].at[piece_of(((y - e + Y) % Y) * 2 + core, h)]
-        return remote(piece, piece, m_s.at[0], m_r.at[c if e else 0, e], at(b, mate))
+        return remote(piece, piece, m_s.at[0], m_r.at[2 * e - 1 + c if e else 0], at(b, mate))
 
     def keys_on():
         return remote(sk.at[slot(G - 1)], pk, p_s.at[0], p_r.at[0], at((b + 1) % B, 0))
 
     def values_on():
-        return remote(sv.at[slot(G - 1)], pv, p_s.at[1], p_r.at[1], at((b + 1) % B, G - 2))
+        return remote(sv.at[slot(G - 1)], pv, p_s.at[0], p_r.at[1], at((b + 1) % B, G - 2))
 
     def values_over():
-        return remote(pv, pv, p_s.at[2], p_r.at[2], at(b, 0))
+        return remote(pv, pv, p_s.at[0], p_r.at[1], at(b, 0))
 
     def block_out(c, d):
         return remote(
@@ -495,7 +495,7 @@
     relay(0, 0)
     def spread(c):
         for e in range(1, Y):
-            all_of(sk.at[pl.ds(0, own_blocks)], m_r.at[c, e]).wait()
+            all_of(sk.at[pl.ds(0, own_blocks)], m_r.at[2 * e - 1 + c]).wait()
         for d in range(1, B):
 
             @when(b + d < B)
@@ -514,7 +514,7 @@
     def _():
         keys_on().start()
 
-    all_of(sk.at[pl.ds(0, 2 * own_blocks)], m_r.at[0, 0]).wait()
+    all_of(sk.at[pl.ds(0, 2 * own_blocks)], m_r.at[0]).wait()
 
     def prev_front(prev_keys, step):
         s = scores(prev_keys[step * ROWS :], qs[step])
@@ -844,9 +844,9 @@
             dma((1,)),
             dma((2, Y - 1, 2)),
             dma((1,)),
-            dma((2, Y)),
-            dma((3,)),
-            dma((3,)),
+            dma((2 * Y - 1,)),
+            dma((1,)),
+            dma((2,)),
             dma((1,)),
             dma((1,)),
             dma((1,)),

time: 18 us -> 18 us (level)
  no operation moved by 1% of the time
where the time goes in v7:
time: 18 us; the launch traced here: 17.8 us
  Pallas kernels  17 us (94%)
  local copies, waits for them, and re-layouts  0.8 us (4%)
    pallas_call x1, Pallas kernels, per_device(): pl.pallas_call(functools.partial(kernel, B, G), out_shape=pltpu.VMEM(quer...  17 us
    unnamed x1, local copies, waits for them, and re-layouts  0.8 us

profile of v7, /device:TPU:24, one launch (start us, length us, event | category | flops | bytes accessed | tf_op | source)
XLA Modules:
  0.0 17.8 jit_solution(12496878592129411200)
XLA Ops:
  0.0 17.0 %shard_map.100 = bf16[512,512]{1,0:T(8,128)(2,1)S(1)} custom-call(s32[16,32]{1,0:T(8,128)} %bitcast.7, bf16[512,512]{1,0:T(8,128)(2,1)} %queries_in.1, bf16[8,64,128]{2,1,0:T(8,128)(2,1)} %bitcast.4, bf16[8,64,128]{2,1,0:T(8,128)(2,1)} %bitcast.5, bf16[4096,256]{1,0:T(8,128)(2,1)} %key_in.1, bf16[256,128]{1,0:T(8,128)(2,1)} %key_out.1, ...), custom_call_target="tpu_custom_call" | custom-call | tf_op jit(solution)/shard_map/pallas_call | solution.py:806
  17.0 0.8 %copy.12 = bf16[512,512]{1,0:T(8,128)(2,1)} copy(bf16[512,512]{1,0:T(8,128)(2,1)S(1)} %shard_map.100) | data formatting | bytes 1048576
